TPU v7x, 32 devices: a whole 2x2x4 slice. The times are simulated.
32 devices in a mesh: px: 4 (over x, core), py: 8 (over z, y).
Axes of the slice: x: 2, y: 2, z: 4, core: 2. Of those that a mesh axis runs over, the one named last changes fastest.
Arguments:
- displacement: float32 [3, 131072], P(None, ('px', 'py')), may hold values from -6 to 6
- disp_prev: float32 [3, 131072], P(None, ('px', 'py')), may hold values from -6 to 6
- nodal_load: float32 [3, 131072], P(None, ('px', 'py')), may hold values from -6 to 6
- nodal_mass: float32 [131072], P(('px', 'py')), may hold values from 1 to 4
- modulus: float32 [16384], P(('px', 'py')), may hold values from 1 to 10
- stiffness: float32 [81, 81], replicated
- connectivity: int32 [27, 16384], P(None, ('px', 'py')), may hold values from 0 to 4607, as said below
- ghost_send: int32 [2, 8192], P(None, ('px', 'py')), may hold values from 0 to 4095
- contact_node: int32 [65536], P(('px', 'py')), may hold values from 0 to 4095
- contact_owner: int32 [65536], P(('px', 'py')), may hold values from 0 to 31, as said below
- pair_ids: int32 [2, 32768], P(None, ('px', 'py')), may hold values from 0 to 4095
- gap_start: float32 [3, 32768], P(None, ('px', 'py')), may hold values from -3 to 3
- penalty: float32 [32768], P(('px', 'py')), may hold values from 0.5 to 2
- friction: float32 [32768], P(('px', 'py')), may hold values from 0.2 to 0.6
- slip_state: int32 [3, 32768], P(None, ('px', 'py')), may hold values 0 or 1
Outputs:
- new_displacement: float32 [3, 131072], P(None, ('px', 'py'))
- acceleration: float32 [3, 131072], P(None, ('px', 'py'))
Inputs may be any that keep to these rules, and one draw needn't show every extreme that they name: `connectivity`: of each device's 512 elements, the first 384 name only the device's own nodes, indices below 4096; the others name own and ghost nodes. `contact_owner`: among the 2048 contact nodes of one device at most 128 name the same owner; one owner is named by exactly 128 nodes of every device.
All inputs are finite; a program needn't handle non-finite values. No bound on the sum of `slip_state` on one device may be relied on, other than what follows from the above.
Results may differ from a plain program's by a relative error of at most 0.0003.
Values sent between devices are 32-bit elements; how exact they have to be, the bound alone decides.
A program may use at most 64 MiB of HBM per device.

v0:
```python
import functools

import jax
import jax.numpy as jnp
from jax import lax
from jax.experimental import pallas as pl
from jax.experimental.pallas import tpu as pltpu
from jax.sharding import PartitionSpec as P

STEPS = 3
LANES = 128
SUBLANES = 8
MESH = pl.DeviceIdType.MESH

time_step_sq = 0.05


def matches(index_row, rows):
    return lax.broadcasted_iota(jnp.int32, (rows, index_row.shape[1]), 0) == index_row


def split(value):
    high = value.astype(jnp.bfloat16)
    return high, (value - high.astype(jnp.float32)).astype(jnp.bfloat16)


def gather_block(table, index, rows, used):
    row_of = lax.shift_right_arithmetic(index, 7)
    lane_of = index & (LANES - 1)
    got = [jnp.zeros((SUBLANES, LANES), jnp.float32)] * 3
    for r in range(used):
        mask = row_of == r
        for c in range(3):
            at = c * rows + r
            line = jnp.broadcast_to(table[at : at + 1, :], (SUBLANES, LANES))
            value = jnp.take_along_axis(line, lane_of, axis=1, mode="promise_in_bounds")
            got[c] = jnp.where(mask, value, got[c])
    return got


def scatter(values, lane_hot, row_index, rows):
    mask = matches(row_index, rows)
    parts = [split(value) for value in values]
    left = jnp.concatenate(
        [jnp.where(mask, parts[c][s].astype(jnp.float32), 0.0) for s in range(2) for c in range(3)],
        axis=0,
    ).astype(jnp.bfloat16)
    return lax.dot_general(
        left, lane_hot, (((1,), (1,)), ((), ())), preferred_element_type=jnp.float32
    )


def kernel(
    dims,
    given_idx,
    lend_idx,
    owner,
    node,
    mod,
    stiff,
    gap0,
    pen,
    fric,
    slip,
    disp,
    prev,
    load,
    mass,
    out_u,
    out_a,
    idx,
    lane_hot,
    stiff_wide,
    ext,
    ue,
    fe,
    acc_e,
    slot_vals,
    ends,
    pair_vals,
    recv_tab,
    cur,
    old,
    box_out,
    box_in,
    halo_out,
    halo_in,
    box_send,
    box_recv,
    halo_send,
    halo_recv,
):
    n_py, n, cap, elnode, lent, width = dims
    px, py = lax.axis_index("px"), lax.axis_index("py")
    me = px * n_py + py

    def place(device):
        return {"px": lax.div(device, n_py), "py": lax.rem(device, n_py)}

    barrier = pltpu.get_barrier_semaphore()

    @pl.loop(1, n)
    def _(d):
        pl.semaphore_signal(
            barrier, inc=1, device_id=place(lax.rem(me + d, n)), device_id_type=MESH
        )

    own_rows = cur.shape[0] // 3
    ext_rows = ext.shape[0] // 3
    slots = slot_vals.shape[1]
    slot_rows = recv_tab.shape[0] // 3
    given = given_idx.shape[0]
    wide = stiff_wide.shape[0] // 3
    lend = wide
    pair_chunks = pen.shape[1] // width
    near, far = lend + 1, lend + 1 + pair_chunks

    def set_row(k, row):
        idx[pl.ds(k, 1), :] = row
        lane_hot[k] = jnp.where(matches(row & (LANES - 1), LANES), 1.0, 0.0).astype(jnp.bfloat16)

    def scatter_row(values, k, rows):
        row = lax.shift_right_arithmetic(idx[pl.ds(k, 1), :], 7)
        return scatter(values, lane_hot[k], row, rows)

    @pl.loop(0, given)
    def _(k):
        set_row(k, given_idx[pl.ds(k, 1), :])

    stiff_wide[...] = jnp.zeros_like(stiff_wide)
    for c in range(3):
        for d in range(3):
            stiff_wide[c * wide : c * wide + elnode, d * wide : d * wide + elnode] = stiff[
                c * elnode : (c + 1) * elnode, d * elnode : (d + 1) * elnode
            ]

    before = (
        lax.broadcasted_iota(jnp.int32, (width, width), 0)
        < lax.broadcasted_iota(jnp.int32, (width, width), 1)
    )
    before = jnp.where(before, 1.0, 0.0).astype(jnp.bfloat16)
    carry = jnp.zeros((n, 1), jnp.float32)
    found = jnp.zeros((2 * slots, width), jnp.float32)
    for j in range(owner.shape[0]):
        target = owner[j : j + 1, :]
        mask = matches(target, n)
        hot = jnp.where(mask, 1.0, 0.0)
        earlier = jnp.dot(hot.astype(jnp.bfloat16), before, preferred_element_type=jnp.float32)
        rank = jnp.sum(jnp.where(mask, earlier + carry, 0.0), axis=0, keepdims=True)
        carry = carry + jnp.sum(hot, axis=1, keepdims=True)
        slot = target * cap + rank.astype(jnp.int32)
        mask = matches(lax.div(slot, width), slots)
        number = node[j : j + 1, :] + 1
        left = jnp.concatenate(
            [
                jnp.where(mask, lax.shift_right_arithmetic(number, 6).astype(jnp.float32), 0.0),
                jnp.where(mask, (number & 63).astype(jnp.float32), 0.0),
            ],
            axis=0,
        ).astype(jnp.bfloat16)
        right = jnp.where(matches(lax.rem(slot, width), width), 1.0, 0.0).astype(jnp.bfloat16)
        found = found + lax.dot_general(
            left, right, (((1,), (1,)), ((), ())), preferred_element_type=jnp.float32
        )
    numbers = (found[:slots] * 64.0 + found[slots:]).astype(jnp.int32) - 1
    for q in range(slots):
        set_row(given + q, numbers[q : q + 1, :])

    cur[...] = disp[...]
    old[...] = prev[...]
    ext[...] = jnp.zeros_like(ext)

    def box_copy(i, d):
        other = lax.rem(me + d, n)
        return pltpu.make_async_remote_copy(
            src_ref=box_out.at[i, other],
            dst_ref=box_in.at[i, me],
            send_sem=box_send.at[i],
            recv_sem=box_recv.at[i],
            device_id=place(other),
            device_id_type=MESH,
        )

    def box_start(i):
        @pl.loop(1, n)
        def _(d):
            box_copy(i, d).start()

        box_in[i, me] = box_out[i, me]

    def box_wait(i):
        every = pl.ds(0, n - 1)
        whole = pltpu.make_async_remote_copy(
            src_ref=box_out.at[i, every],
            dst_ref=box_in.at[i, every],
            send_sem=box_send.at[i],
            recv_sem=box_recv.at[i],
            device_id=place(lax.rem(me + 1, n)),
            device_id_type=MESH,
        )
        whole.wait()

    def halo_copies(i):
        copies = []
        for side, step in ((0, n - 1), (1, 1)):
            copies.append(
                pltpu.make_async_remote_copy(
                    src_ref=halo_out.at[i, side],
                    dst_ref=halo_in.at[i, 1 - side],
                    send_sem=halo_send.at[i, side],
                    recv_sem=halo_recv.at[i, 1 - side],
                    device_id=place(lax.rem(me + step, n)),
                    device_id_type=MESH,
                )
            )
        return copies

    def halo_start(i):
        for copy in halo_copies(i):
            copy.start()

    def halo_wait(i):
        for copy in halo_copies(i):
            copy.wait()

    def halo_side(i, side, c):
        inside = me > 0 if side == 0 else me < n - 1
        return jnp.where(inside, halo_in[i, side, c : c + 1, :], 0.0)

    lent_rows = lent // LANES
    blocks = width // LANES

    def gather_rows(table, first, count, rows, used, store):
        @pl.loop(0, count // SUBLANES * blocks, unroll=2)
        def _(i):
            row = pl.multiple_of(lax.div(i, blocks) * SUBLANES, SUBLANES)
            lane = pl.multiple_of(lax.rem(i, blocks) * LANES, LANES)
            index = idx[pl.ds(first + row, SUBLANES), pl.ds(lane, LANES)]
            for c, value in enumerate(gather_block(table, index, rows, used)):
                store(c, pl.ds(row, SUBLANES), pl.ds(lane, LANES), value)

    def slot_store(c, rows, lanes, value):
        slot_vals[c, rows, lanes] = value

    def element_store(c, rows, lanes, value):
        ue[c, rows, lanes] = value

    def end_store(c, rows, lanes, value):
        ends[c, rows, lanes] = value

    for step in range(STEPS):
        going, back = 2 * step, 2 * step + 1
        lending = gather_block(cur, lend_idx[...], own_rows, own_rows)
        for c in range(3):
            for side in range(2):
                for r in range(lent_rows):
                    at = side * lent_rows + r
                    halo_out[going, side, c : c + 1, r * LANES : (r + 1) * LANES] = lending[c][
                        at : at + 1
                    ]
        if step == 0:
            pl.semaphore_wait(barrier, n - 1)
        halo_start(going)

        gather_rows(cur, given, slots, own_rows, own_rows, slot_store)

        for o in range(n):
            r, l = divmod(o * cap, width)
            for c in range(3):
                box_out[going, o, c : c + 1, :] = slot_vals[c, r : r + 1, l : l + cap]
        box_start(going)

        halo_wait(going)
        for c in range(3):
            ext[c * ext_rows : c * ext_rows + own_rows, :] = cur[c * own_rows : (c + 1) * own_rows, :]
            for side in range(2):
                ghosts = halo_side(going, side, c)
                for r in range(lent_rows):
                    at = c * ext_rows + own_rows + side * lent_rows + r
                    ext[at : at + 1, :] = ghosts[:, r * LANES : (r + 1) * LANES]

        gather_rows(ext, 0, wide, ext_rows, own_rows + 2 * lent_rows, element_store)

        box_wait(going)
        for g in range(n):
            r, l = divmod(g * cap, LANES)
            for c in range(3):
                at = c * slot_rows + r
                recv_tab[at : at + 1, l : l + cap] = box_in[going, g, c : c + 1, :]
        gather_rows(recv_tab, lend, SUBLANES, slot_rows, slot_rows, end_store)
        total = jnp.zeros((6 * slot_rows, LANES), jnp.float32)
        for p in range(pair_chunks):
            cols = slice(p * width, (p + 1) * width)
            low = [ends[c, 1 + p : 2 + p, :] for c in range(3)]
            high = [ends[c, 1 + pair_chunks + p : 2 + pair_chunks + p, :] for c in range(3)]
            gap = [gap0[c : c + 1, cols] + high[c] - low[c] for c in range(3)]
            normal = pen[:, cols] * jnp.maximum(-gap[2], 0.0)
            length = jnp.sqrt(gap[0] * gap[0] + gap[1] * gap[1] + 0.01)
            slipping = slip[step : step + 1, cols] == 1
            factor = jnp.where(
                slipping, -fric[:, cols] * normal / length, -0.5 * pen[:, cols]
            )
            force = [factor * gap[0], factor * gap[1], normal]
            total = total + scatter_row(force, far + p, slot_rows)
            total = total - scatter_row(force, near + p, slot_rows)
        pair_vals[...] = total[: 3 * slot_rows] + total[3 * slot_rows :]
        for g in range(n):
            r, l = divmod(g * cap, LANES)
            for c in range(3):
                at = c * slot_rows + r
                box_out[back, g, c : c + 1, :] = pair_vals[at : at + 1, l : l + cap]
        box_start(back)

        fe[...] = (
            jnp.dot(
                stiff_wide[...],
                ue[...].reshape(3 * wide, width),
                precision=lax.Precision.HIGHEST,
                preferred_element_type=jnp.float32,
            )
            * mod[...]
        )
        acc_e[...] = jnp.zeros_like(acc_e)

        some = next(f for f in (9, 3, 1) if elnode % f == 0)

        @pl.loop(0, elnode // some)
        def _(group):
            total = acc_e[...]
            for i in range(some):
                k = group * some + i
                values = [fe[pl.ds(c * wide + k, 1), :] for c in range(3)]
                total = total + scatter_row(values, k, ext_rows)
            acc_e[...] = total

        ext[...] = acc_e[: 3 * ext_rows] + acc_e[3 * ext_rows :]
        for c in range(3):
            for side in range(2):
                for r in range(lent_rows):
                    at = c * ext_rows + own_rows + side * lent_rows + r
                    halo_out[back, side, c : c + 1, r * LANES : (r + 1) * LANES] = ext[at : at + 1, :]
        halo_start(back)

        box_wait(back)
        for o in range(n):
            r, l = divmod(o * cap, width)
            for c in range(3):
                slot_vals[c, r : r + 1, l : l + cap] = box_in[back, o, c : c + 1, :]
        contact = jnp.zeros((6 * own_rows, LANES), jnp.float32)
        for q in range(slots):
            values = [slot_vals[c, q : q + 1, :] for c in range(3)]
            contact = contact + scatter_row(values, given + q, own_rows)

        halo_wait(back)
        values = [
            jnp.concatenate([halo_side(back, 0, c), halo_side(back, 1, c)], axis=1) for c in range(3)
        ]
        total = contact - scatter_row(values, lend, own_rows)
        total = total[: 3 * own_rows] + total[3 * own_rows :]
        for c in range(3):
            rows = slice(c * own_rows, (c + 1) * own_rows)
            internal = ext[c * ext_rows : c * ext_rows + own_rows, :]
            acceleration = (load[rows, :] - internal + total[rows]) / mass[...]
            now = cur[rows, :]
            later = 2.0 * now - old[rows, :] + time_step_sq * acceleration
            old[rows, :] = now
            cur[rows, :] = later
            if step == STEPS - 1:
                out_u[rows, :] = later
                out_a[rows, :] = acceleration


def on_device(
    n_py,
    displacement,
    disp_prev,
    nodal_load,
    nodal_mass,
    modulus,
    stiffness,
    connectivity,
    ghost_send,
    contact_node,
    contact_owner,
    pair_ids,
    gap_start,
    penalty,
    friction,
    slip_state,
):
    n = lax.axis_size(("px", "py"))
    cap = 2 * contact_node.shape[0] // n
    elnode, width = connectivity.shape
    nodes = displacement.shape[1]
    lent = ghost_send.shape[1]
    own_rows = nodes // LANES
    ext_rows = -(-(own_rows + 2 * lent // LANES) // SUBLANES) * SUBLANES
    slots = n * cap // width
    slot_rows = n * cap // LANES
    wide = -(-elnode // SUBLANES) * SUBLANES
    pairs = pair_ids.reshape(-1, width)
    idx = jnp.concatenate(
        [
            jnp.pad(connectivity, ((0, wide - elnode), (0, 0)), constant_values=-1),
            ghost_send.reshape(1, 2 * lent),
            jnp.pad(pairs, ((0, -(1 + pairs.shape[0]) % SUBLANES), (0, 0)), constant_values=-1),
        ],
        axis=0,
    )
    lend_idx = ghost_send.reshape(-1, LANES)
    lend_idx = jnp.pad(lend_idx, ((0, -lend_idx.shape[0] % SUBLANES), (0, 0)), constant_values=-1)
    chunks = idx.shape[0] + slots
    flat = (3 * own_rows, LANES)
    vmem = pl.BlockSpec(memory_space=pltpu.VMEM)
    f32, bf16 = jnp.float32, jnp.bfloat16
    dma = pltpu.SemaphoreType.DMA
    new_u, acc = pl.pallas_call(
        functools.partial(kernel, (n_py, n, cap, elnode, lent, width)),
        out_shape=[jax.ShapeDtypeStruct(flat, f32)] * 2,
        in_specs=[vmem] * 14,
        out_specs=[vmem] * 2,
        scratch_shapes=[
            pltpu.VMEM((chunks, width), jnp.int32),
            pltpu.VMEM((chunks, LANES, width), bf16),
            pltpu.VMEM((3 * wide, 3 * wide), f32),
            pltpu.VMEM((3 * ext_rows, LANES), f32),
            pltpu.VMEM((3, wide, width), f32),
            pltpu.VMEM((3 * wide, width), f32),
            pltpu.VMEM((6 * ext_rows, LANES), f32),
            pltpu.VMEM((3, slots, width), f32),
            pltpu.VMEM((3, SUBLANES, width), f32),
            pltpu.VMEM((3 * slot_rows, LANES), f32),
            pltpu.VMEM((3 * slot_rows, LANES), f32),
            pltpu.VMEM(flat, f32),
            pltpu.VMEM(flat, f32),
            pltpu.VMEM((2 * STEPS, n, 3, cap), f32),
            pltpu.VMEM((2 * STEPS, n, 3, cap), f32),
            pltpu.VMEM((2 * STEPS, 2, 3, lent), f32),
            pltpu.VMEM((2 * STEPS, 2, 3, lent), f32),
            dma((2 * STEPS,)),
            dma((2 * STEPS,)),
            dma((2 * STEPS, 2)),
            dma((2 * STEPS, 2)),
        ],
        compiler_params=pltpu.CompilerParams(
            collective_id=0, has_side_effects=True, vmem_limit_bytes=48 * 1024 * 1024
        ),
        name="contact_steps",
    )(
        idx,
        lend_idx,
        contact_owner.reshape(-1, width),
        contact_node.reshape(-1, width),
        modulus.reshape(1, -1),
        stiffness,
        gap_start,
        penalty.reshape(1, -1),
        friction.reshape(1, -1),
        slip_state,
        displacement.reshape(flat),
        disp_prev.reshape(flat),
        nodal_load.reshape(flat),
        nodal_mass.reshape(-1, LANES),
    )
    return new_u.reshape(displacement.shape), acc.reshape(displacement.shape)


def solution(mesh):
    both = ("px", "py")
    row, cols = P(both), P(None, both)
    return jax.shard_map(
        functools.partial(on_device, mesh.shape["py"]),
        mesh=mesh,
        in_specs=(cols, cols, cols, row, row, P(), cols, cols, row, row, cols, cols, row, row, cols),
        out_specs=(cols, cols),
        check_vma=False,
    )
```

profile of v0, /device:TPU:0, one launch (start us, length us, event | category | flops | bytes accessed | tf_op | source)
XLA Modules:
  0.0 60.4 jit_solution(18084376100936995614)
XLA Ops:
  0.6 0.0 copy-start.7
  0.6 0.7 %copy.17 = s32[1,1,2,256]{3,1,2,0:T(1,128)S(1)} copy(s32[1,1,2,256]{3,2,1,0:T(2,128)} %bitcast.12) | data formatting | bytes 4096
  1.4 0.7 %reshape.48 = s32[4,128]{1,0:T(4,128)S(1)} reshape(s32[2,256]{1,0:T(2,128)} %param.22) | data formatting | bytes 4096 | tf_op jit(solution)/shard_map/reshape | solution.py:410
  2.1 0.7 %reshape.50.node = s32[4,512]{1,0:T(4,128)S(1)} reshape(s32[2048]{0:T(1024)} %param.23) | data formatting | bytes 16384 | tf_op jit(solution)/shard_map/reshape | solution.py:453
  2.8 0.7 %reshape.49.owner = s32[4,512]{1,0:T(4,128)S(1)} reshape(s32[2048]{0:T(1024)} %param.24) | data formatting | bytes 16384 | tf_op jit(solution)/shard_map/reshape | solution.py:452
  3.5 0.0 copy-start.8
  3.5 0.7 %reshape.47 = s32[4,512]{1,0:T(4,128)S(1)} reshape(s32[2,1024]{1,0:T(2,128)} %param.25) | data formatting | bytes 16384 | tf_op jit(solution)/shard_map/reshape | solution.py:401
  4.2 0.0 copy-done.7
  4.3 0.0 copy-done.8
  4.3 0.0 copy-start.9
  4.4 0.8 %copy-done.9 = f32[3,4096]{1,0:T(4,128)S(1)} copy-done((f32[3,4096]{1,0:T(4,128)S(1)}, f32[3,4096]{1,0:T(4,128)}, u32[]{:S(2)}) %copy-start.9) | copy-done | bytes 49176
  5.1 0.0 copy-start.10
  5.2 0.8 %copy-done.10 = s32[27,512]{1,0:T(8,128)S(1)} copy-done((s32[27,512]{1,0:T(8,128)S(1)}, s32[27,512]{1,0:T(8,128)}, u32[]{:S(2)}) %copy-start.10) | copy-done | bytes 55320
  6.0 0.0 copy-start
  6.0 0.0 copy-start.1
  6.0 0.0 copy-start.2
  6.0 0.0 copy-start.3
  6.0 0.0 copy-start.4
  6.0 0.0 copy-start.5
  6.0 0.0 copy-start.6
  6.1 0.7 %copy-done = f32[81,81]{1,0:T(8,128)S(1)} copy-done((f32[81,81]{1,0:T(8,128)S(1)}, f32[81,81]{1,0:T(8,128)}, u32[]{:S(2)}) %copy-start) | copy-done | bytes 26268
  6.8 0.0 copy-done.1
  6.8 0.0 copy-done.2
  6.8 0.0 copy-done.3
  6.8 0.0 copy-done.4
  6.8 0.0 copy-done.5
  6.8 0.0 copy-done.6
  6.8 52.3 %contact_steps.1 = (f32[96,128]{1,0:T(8,128)S(1)}, f32[96,128]{1,0:T(8,128)S(1)}) custom-call(s32[40,512]{1,0:T(8,128)S(1)} %select_add_fusion.given_idx, s32[8,128]{1,0:T(8,128)S(1)} %pad.14.lend_idx, s32[4,512]{1,0:T(4,128)S(1)} %reshape.49.owner, s32[4,512]{1,0:T(4,128)S(1)} %reshape.50.node, f32[1,512]{1,0:T(1,128)S(1)} %bitcast.10, ...), custom_call_target="tpu_custom_call" | custom-call | tf_op jit(solution)/shard_map/contact_steps/pallas_call | solution.py:417
  59.1 0.7 %reshape.58 = f32[3,4096]{1,0:T(4,128)} reshape(f32[96,128]{1,0:T(8,128)S(1)} %get-tuple-element.4) | data formatting | bytes 98304 | tf_op jit(solution)/shard_map/reshape | solution.py:465
  59.7 0.7 %reshape.59 = f32[3,4096]{1,0:T(4,128)} reshape(f32[96,128]{1,0:T(8,128)S(1)} %get-tuple-element.5) | data formatting | bytes 98304 | tf_op jit(solution)/shard_map/reshape | solution.py:465
  (5 shorter events, 0.1 us)
Async XLA Ops:
  0.6 3.6 %copy-start.7 = (f32[3,4096]{1,0:T(4,128)S(1)}, f32[3,4096]{1,0:T(4,128)}, u32[]{:S(2)}) copy-start(f32[3,4096]{1,0:T(4,128)} %param.15) | copy-start | bytes 147460
  3.5 0.8 %copy-start.8 = (f32[3,4096]{1,0:T(4,128)S(1)}, f32[3,4096]{1,0:T(4,128)}, u32[]{:S(2)}) copy-start(f32[3,4096]{1,0:T(4,128)} %param.16) | copy-start | bytes 147460
  4.3 0.8 %copy-start.9 = (f32[3,4096]{1,0:T(4,128)S(1)}, f32[3,4096]{1,0:T(4,128)}, u32[]{:S(2)}) copy-start(f32[3,4096]{1,0:T(4,128)} %param.17) | copy-start | bytes 147460
  5.1 0.8 %copy-start.10 = (s32[27,512]{1,0:T(8,128)S(1)}, s32[27,512]{1,0:T(8,128)}, u32[]{:S(2)}) copy-start(s32[27,512]{1,0:T(8,128)} %param.21) | copy-start | bytes 165892
  6.0 0.8 %copy-start = (f32[81,81]{1,0:T(8,128)S(1)}, f32[81,81]{1,0:T(8,128)}, u32[]{:S(2)}) copy-start(f32[81,81]{1,0:T(8,128)} %stiff.1) | copy-start | bytes 78736
  6.0 0.8 %copy-start.1 = (f32[3,1024]{1,0:T(4,128)S(1)}, f32[3,1024]{1,0:T(4,128)}, u32[]{:S(2)}) copy-start(f32[3,1024]{1,0:T(4,128)} %gap0.1) | copy-start | bytes 36868
  6.0 0.8 %copy-start.2 = (s32[3,1024]{1,0:T(4,128)S(1)}, s32[3,1024]{1,0:T(4,128)}, u32[]{:S(2)}) copy-start(s32[3,1024]{1,0:T(4,128)} %slip.1) | copy-start | bytes 36868
  6.0 0.8 %copy-start.3 = (f32[4096]{0:T(1024)S(1)}, f32[4096]{0:T(1024)}, u32[]{:S(2)}) copy-start(f32[4096]{0:T(1024)} %param.18) | copy-start | bytes 49156
  6.0 0.8 %copy-start.4 = (f32[1024]{0:T(1024)S(1)}, f32[1024]{0:T(1024)}, u32[]{:S(2)}) copy-start(f32[1024]{0:T(1024)} %param.27) | copy-start | bytes 12292
  6.0 0.8 %copy-start.5 = (f32[1024]{0:T(1024)S(1)}, f32[1024]{0:T(1024)}, u32[]{:S(2)}) copy-start(f32[1024]{0:T(1024)} %param.28) | copy-start | bytes 12292
  6.0 0.8 %copy-start.6 = (f32[512]{0:T(512)S(1)}, f32[512]{0:T(512)}, u32[]{:S(2)}) copy-start(f32[512]{0:T(512)} %param.19) | copy-start | bytes 6148
where the time goes:
time: 60.8 us; the launch traced here: 60.4 us
  Pallas kernels  52.3 us (86%)
  local copies, waits for them, and re-layouts  7.38 us (12%)
  between operations  0.73 us (1%)
    pallas_call x1, Pallas kernels, on_device(): pl.pallas_call(functools.partial(kernel, (n_py, n, cap, elnode, lent, wid...  52.3 us
    unnamed x23, local copies, waits for them, and re-layouts  3.11 us
    reshape x2, local copies, waits for them, and re-layouts, on_device(): return (new_u.reshape(displacement.shape), acc.reshape(displacement.shape))  1.3 us

commit v1 on v0

v1 whole, which is shorter than its diff:
```python
import functools

import jax
import jax.numpy as jnp
from jax import lax
from jax.experimental import pallas as pl
from jax.experimental.pallas import tpu as pltpu
from jax.sharding import PartitionSpec as P

STEPS = 3
LANES = 128
SUBLANES = 8
PLANES = 4
MESH = pl.DeviceIdType.MESH

time_step_sq = 0.05


def matches(index_row, rows):
    return lax.broadcasted_iota(jnp.int32, (rows, index_row.shape[1]), 0) == index_row


def split(value):
    high = value.astype(jnp.bfloat16).astype(jnp.float32)
    return high, value - high


def contract(left, right):
    return lax.dot_general(
        left, right, (((1,), (1,)), ((), ())), preferred_element_type=jnp.float32
    )


def spread(parts, row_index, rows):
    mask = matches(row_index, rows)
    return jnp.concatenate([jnp.where(mask, part, 0.0) for part in parts], axis=0).astype(
        jnp.bfloat16
    )


def pick(got, lines, row_of, lane_of, r):
    mask = row_of == r
    for c in range(3):
        line = jnp.broadcast_to(lines[c], (SUBLANES, LANES))
        value = jnp.take_along_axis(line, lane_of, axis=1, mode="promise_in_bounds")
        got[c] = jnp.where(mask, value, got[c])


def blank():
    return [jnp.zeros((SUBLANES, LANES), jnp.float32)] * 3


def places_of(index):
    return lax.shift_right_arithmetic(index, 7), index & (LANES - 1)


def kernel(
    dims,
    disp_hbm,
    prev_hbm,
    load_hbm,
    mass_hbm,
    mod_hbm,
    stiff_hbm,
    conn_hbm,
    ghost_hbm,
    node_hbm,
    owner_hbm,
    pair_hbm,
    gap_hbm,
    pen_hbm,
    fric_hbm,
    slip_hbm,
    out_u,
    out_a,
    disp,
    prev,
    load,
    mass,
    mod,
    stiff,
    conn,
    ghost,
    node,
    owner,
    pair,
    gap0,
    pen,
    fric,
    slip,
    row_of_entry,
    lane_hot,
    stiff_parts,
    slot_idx,
    pair_idx,
    lend_idx,
    ue,
    fe,
    acc_e,
    cur,
    old,
    loads,
    gaps,
    slips,
    box_out,
    box_in,
    halo_out,
    halo_in,
    in_sem,
    box_send,
    box_recv,
    halo_send,
    halo_recv,
):
    n_py, n, cap, elnode, lent, width, inner = dims
    px, py = lax.axis_index("px"), lax.axis_index("py")
    me = px * n_py + py

    def place(device):
        return {"px": lax.div(device, n_py), "py": lax.rem(device, n_py)}

    fills = [
        pltpu.make_async_copy(source, target, in_sem.at[i])
        for i, (source, target) in enumerate(
            [
                (owner_hbm, owner),
                (node_hbm, node),
                (disp_hbm, disp),
                (ghost_hbm, ghost),
                (conn_hbm, conn),
                (pair_hbm, pair),
                (stiff_hbm, stiff),
                (mod_hbm, mod),
                (gap_hbm, gap0),
                (slip_hbm, slip),
                (pen_hbm, pen),
                (fric_hbm, fric),
                (prev_hbm, prev),
                (load_hbm, load),
                (mass_hbm, mass),
            ]
        )
    ]
    for fill in fills:
        fill.start()

    barrier = pltpu.get_barrier_semaphore()

    @pl.loop(1, n)
    def _(d):
        pl.semaphore_signal(
            barrier, inc=1, device_id=place(lax.rem(me + d, n)), device_id_type=MESH
        )

    per_plane = n // PLANES
    rows_y = n_py // PLANES
    z, y = lax.div(py, rows_y), lax.rem(py, rows_y)
    half = lax.div(z, 2)
    plane_at = [3 * (1 - half), 2 - half, 1 + 4 * half - z, z]
    my_q = px * rows_y + y
    my_p = (PLANES - 1) * per_plane + my_q

    def device_at(j, q):
        return lax.div(q, rows_y) * n_py + plane_at[j] * rows_y + lax.rem(q, rows_y)

    own_rows = cur.shape[0] // 3
    slot_rows = slot_idx.shape[0]
    plane_rows = slot_rows // PLANES
    per_row = LANES // cap
    wide = ue.shape[0] // 3
    lent_rows = lent // LANES
    ghost_rows = 2 * lent_rows
    chunks = width // LANES
    pair_rows = pair_idx.shape[0] // 2
    pair_groups = pair_rows // chunks
    slot_groups = slot_rows // chunks
    lend = elnode
    near, far = lend + 1, lend + 1 + pair_groups
    first_slot = far + pair_groups

    def set_row(k, row):
        row_of_entry[pl.ds(k, 1), :] = lax.shift_right_arithmetic(row, 7)
        lane_hot[k] = jnp.where(matches(row & (LANES - 1), LANES), 1.0, 0.0).astype(jnp.bfloat16)

    def flat_row(table, first):
        return jnp.concatenate([table[first + i : first + i + 1, :] for i in range(chunks)], axis=1)

    for fill in fills[:2]:
        fill.wait()

    from_lane = lax.broadcasted_iota(jnp.int32, (LANES, 2 * LANES), 0)
    to_lane = lax.broadcasted_iota(jnp.int32, (LANES, 2 * LANES), 1)
    before = jnp.where(from_lane < to_lane, 1.0, 0.0).astype(jnp.bfloat16)
    target = owner[...]
    target_py = lax.rem(target, n_py)
    target_z = lax.div(target_py, rows_y)
    target_j = jnp.where(
        target_z == plane_at[0],
        0,
        jnp.where(target_z == plane_at[1], 1, jnp.where(target_z == plane_at[2], 2, 3)),
    )
    spot = target_j * per_plane + lax.div(target, n_py) * rows_y + lax.rem(target_py, rows_y)
    pieces = owner.shape[0]
    hot = [jnp.where(matches(spot[i : i + 1, :], n), 1.0, 0.0) for i in range(pieces)]
    counts = jnp.dot(
        jnp.concatenate(hot, axis=0).astype(jnp.bfloat16),
        before,
        preferred_element_type=jnp.float32,
    )
    carry = jnp.zeros((n, LANES), jnp.float32)
    ranks = []
    for i in range(pieces):
        earlier = counts[i * n : (i + 1) * n, :LANES]
        ranks.append(jnp.sum(hot[i] * (earlier + carry), axis=0, keepdims=True))
        carry = carry + counts[i * n : (i + 1) * n, LANES:]
    found = jnp.zeros((2 * slot_rows, LANES), jnp.float32)
    for first in range(0, pieces, chunks):
        lefts, rights = [], []
        for i in range(first, first + chunks):
            number = node[i : i + 1, :] + 1
            slot = spot[i : i + 1, :] * cap + ranks[i].astype(jnp.int32)
            parts = [
                lax.shift_right_arithmetic(number, 6).astype(jnp.float32),
                (number & 63).astype(jnp.float32),
            ]
            lefts.append(spread(parts, lax.shift_right_arithmetic(slot, 7), slot_rows))
            rights.append(
                jnp.where(matches(slot & (LANES - 1), LANES), 1.0, 0.0).astype(jnp.bfloat16)
            )
        found = found + contract(
            jnp.concatenate(lefts, axis=1), jnp.concatenate(rights, axis=1)
        )
    slot_idx[...] = (found[:slot_rows] * 64.0 + found[slot_rows:]).astype(jnp.int32) - 1

    for fill in fills[2:4]:
        fill.wait()

    def to_rows(table, source, rows):
        for c in range(3):
            for r in range(rows):
                table[c * rows + r : c * rows + r + 1, :] = source[
                    c : c + 1, r * LANES : (r + 1) * LANES
                ]

    to_rows(cur, disp, own_rows)
    lend_idx[...] = jnp.full_like(lend_idx, -1)
    for side in range(2):
        for r in range(lent_rows):
            at = side * lent_rows + r
            lend_idx[at : at + 1, :] = ghost[side : side + 1, r * LANES : (r + 1) * LANES]

    def box_copy(i, there, spot_out):
        return pltpu.make_async_remote_copy(
            src_ref=box_out.at[i, spot_out],
            dst_ref=box_in.at[i, me],
            send_sem=box_send.at[i],
            recv_sem=box_recv.at[i, z],
            device_id=place(there),
            device_id_type=MESH,
        )

    def box_bytes(i, count, plane):
        every = pl.ds(0, count)
        return pltpu.make_async_remote_copy(
            src_ref=box_out.at[i, every],
            dst_ref=box_in.at[i, every],
            send_sem=box_send.at[i],
            recv_sem=box_recv.at[i, plane],
            device_id=place(lax.rem(me + 1, n)),
            device_id_type=MESH,
        )

    def box_start(i, j, by_device):
        for d in range(1 if j == PLANES - 1 else 0, per_plane):
            q = lax.rem(my_q + d, per_plane)
            there = device_at(j, q)
            box_copy(i, there, there if by_device else j * per_plane + q).start()

    def box_wait(i, j):
        own = 1 if j == PLANES - 1 else 0
        box_bytes(i, per_plane - own, plane_at[j]).wait_recv()

    def halo_copies(i):
        copies = []
        for side, step in ((0, n - 1), (1, 1)):
            copies.append(
                pltpu.make_async_remote_copy(
                    src_ref=halo_out.at[i, side],
                    dst_ref=halo_in.at[i, 1 - side],
                    send_sem=halo_send.at[i, side],
                    recv_sem=halo_recv.at[i, 1 - side],
                    device_id=place(lax.rem(me + step, n)),
                    device_id_type=MESH,
                )
            )
        return copies

    def halo_start(i):
        for copy in halo_copies(i):
            copy.start()

    def halo_wait(i):
        for copy in halo_copies(i):
            copy.wait_recv()

    def halo_side(i, side, c):
        inside = me > 0 if side == 0 else me < n - 1
        return jnp.where(inside, halo_in[i, side, c : c + 1, :], 0.0)

    def box_row(i, devices):
        boxes = [box_in[i, device] for device in devices]
        return boxes[0] if per_row == 1 else jnp.concatenate(boxes, axis=1)

    def table_lines(table, rows, r):
        return [table[c * rows + r : c * rows + r + 1, :] for c in range(3)]

    for step in range(STEPS):
        going, back = 2 * step, 2 * step + 1

        row_of, lane_of = places_of(lend_idx[...])
        got = blank()
        for r in range(own_rows):
            pick(got, table_lines(cur, own_rows, r), row_of, lane_of, r)
        for c in range(3):
            for side in range(2):
                for r in range(lent_rows):
                    at = side * lent_rows + r
                    halo_out[going, side, c : c + 1, r * LANES : (r + 1) * LANES] = got[c][
                        at : at + 1
                    ]
        if step == 0:
            pl.semaphore_wait(barrier, n - 1)
        halo_start(going)

        for j in range(PLANES):
            row_of, lane_of = places_of(slot_idx[j * plane_rows : (j + 1) * plane_rows, :])
            got = blank()
            for r in range(own_rows):
                pick(got, table_lines(cur, own_rows, r), row_of, lane_of, r)
            for q in range(per_plane):
                r, l = divmod(q * cap, LANES)
                for c in range(3):
                    box_out[going, j * per_plane + q, c : c + 1, :] = got[c][
                        r : r + 1, l : l + cap
                    ]
            box_start(going, j, False)
        box_in[going, me] = box_out[going, my_p]

        if step == 0:
            for fill in fills[4:]:
                fill.wait()

            @pl.loop(0, elnode)
            def _(k):
                set_row(k, conn[pl.ds(k, 1), :])

            for i in range(2):
                for r in range(pair_rows):
                    pair_idx[i * pair_rows + r : i * pair_rows + r + 1, :] = pair[
                        i : i + 1, r * LANES : (r + 1) * LANES
                    ]
            for i, first in ((0, near), (1, far)):
                for h in range(pair_groups):
                    set_row(first + h, pair[i : i + 1, h * width : (h + 1) * width])
            set_row(lend, flat_row(lend_idx, 0))
            to_rows(gaps, gap0, pair_rows)
            to_rows(slips, slip, pair_rows)
            to_rows(old, prev, own_rows)
            to_rows(loads, load, own_rows)
            ue[...] = jnp.zeros_like(ue)
            stiff_parts[...] = jnp.zeros_like(stiff_parts)
            for c in range(3):
                for d in range(3):
                    block = stiff[c * elnode : (c + 1) * elnode, d * elnode : (d + 1) * elnode]
                    high, low = split(block)
                    for at, part in ((0, high), (1, high), (2, low)):
                        start = (3 * at + d) * wide
                        stiff_parts[c * wide : c * wide + elnode, start : start + elnode] = part

        def forces(cols):
            high, low = split(ue[:, cols])
            right = jnp.concatenate([high, low, high], axis=0).astype(jnp.bfloat16)
            left = stiff_parts[...].astype(jnp.bfloat16)
            product = jnp.dot(left, right, preferred_element_type=jnp.float32) * mod[:, cols]
            high, low = split(product)
            fe[0, :, cols] = high
            fe[1, :, cols] = low

        tops = [min(k, elnode - SUBLANES) for k in range(0, elnode, SUBLANES)]

        @pl.loop(0, chunks)
        def _(i):
            lanes = pl.ds(pl.multiple_of(i * LANES, LANES), LANES)
            for top in tops:
                row_of, lane_of = places_of(conn[top : top + SUBLANES, lanes])
                got = blank()
                for r in range(own_rows):
                    pick(got, table_lines(cur, own_rows, r), row_of, lane_of, r)
                for c in range(3):
                    ue[c * wide + top : c * wide + top + SUBLANES, lanes] = got[c]

        forces(slice(0, inner))

        pair_at = [places_of(pair_idx[i * pair_rows : (i + 1) * pair_rows, :]) for i in range(2)]
        ends = [blank(), blank()]

        def pair_pick(j):
            for q in range(0, per_plane, per_row):
                devices = [device_at(j, q + t) for t in range(per_row)]
                box = box_row(going, devices)
                lines = [box[c : c + 1, :] for c in range(3)]
                row = lax.div(devices[0], per_row)
                for i in range(2):
                    pick(ends[i], lines, *pair_at[i], row)

        for j in range(PLANES - 1, 0, -1):
            box_wait(going, j)
            pair_pick(j)

        halo_wait(going)
        ghosts = [[halo_side(going, side, c) for c in range(3)] for side in range(2)]
        for top in tops:
            row_of, lane_of = places_of(conn[top : top + SUBLANES, inner:])
            for b in range((width - inner) // LANES):
                lanes = slice(b * LANES, (b + 1) * LANES)
                spots = slice(inner + b * LANES, inner + (b + 1) * LANES)
                got = [ue[c * wide + top : c * wide + top + SUBLANES, spots] for c in range(3)]
                for side in range(2):
                    for r in range(lent_rows):
                        lines = [
                            ghosts[side][c][:, r * LANES : (r + 1) * LANES] for c in range(3)
                        ]
                        at = own_rows + side * lent_rows + r
                        pick(got, lines, row_of[:, lanes], lane_of[:, lanes], at)
                for c in range(3):
                    ue[c * wide + top : c * wide + top + SUBLANES, spots] = got[c]
        forces(slice(inner, width))

        edge = jnp.zeros((6 * ghost_rows, LANES), jnp.float32)
        for first in range(0, elnode, chunks):
            lefts, rights = [], []
            for k in range(first, min(first + chunks, elnode)):
                row = row_of_entry[k : k + 1, inner:] - own_rows
                parts = [
                    fe[s, c * wide + k : c * wide + k + 1, inner:] for s in range(2) for c in range(3)
                ]
                lefts.append(spread(parts, row, ghost_rows))
                rights.append(lane_hot[k, :, inner:])
            edge = edge + contract(
                jnp.concatenate(lefts, axis=1), jnp.concatenate(rights, axis=1)
            )
        edge = edge[: 3 * ghost_rows] + edge[3 * ghost_rows :]
        for c in range(3):
            for side in range(2):
                for r in range(lent_rows):
                    at = c * ghost_rows + side * lent_rows + r
                    halo_out[back, side, c : c + 1, r * LANES : (r + 1) * LANES] = edge[at : at + 1]
        halo_start(back)

        box_wait(going, 0)
        pair_pick(0)
        gap = [
            gaps[c * pair_rows : (c + 1) * pair_rows, :] + ends[1][c] - ends[0][c] for c in range(3)
        ]
        normal = pen[...] * jnp.maximum(-gap[2], 0.0)
        length = jnp.sqrt(gap[0] * gap[0] + gap[1] * gap[1] + 0.01)
        slipping = slips[step * pair_rows : (step + 1) * pair_rows, :] == 1
        factor = jnp.where(slipping, -fric[...] * normal / length, -0.5 * pen[...])
        force = [factor * gap[0], factor * gap[1], normal]
        halves = [split(value) for value in force]
        total = jnp.zeros((6 * slot_rows, LANES), jnp.float32)
        for sign, first in ((1.0, far), (-1.0, near)):
            for h in range(pair_groups):
                parts = [
                    flat_row(sign * halves[c][s], h * chunks) for s in range(2) for c in range(3)
                ]
                k = first + h
                total = total + contract(
                    spread(parts, row_of_entry[k : k + 1, :], slot_rows), lane_hot[k]
                )
        total = total[: 3 * slot_rows] + total[3 * slot_rows :]
        for g in range(n):
            r, l = divmod(g * cap, LANES)
            for c in range(3):
                at = c * slot_rows + r
                box_out[back, g, c : c + 1, :] = total[at : at + 1, l : l + cap]
        for j in range(PLANES):
            box_start(back, j, True)
        box_in[back, me] = box_out[back, me]

        if step == 0:
            for m in range(slot_groups):
                set_row(first_slot + m, flat_row(slot_idx, m * chunks))

        acc_e[...] = jnp.zeros_like(acc_e)
        some = next(f for f in (9, 3, 1) if elnode % f == 0)

        @pl.loop(0, elnode // some)
        def _(group):
            total = acc_e[...]
            for i in range(some):
                k = group * some + i
                parts = [
                    fe[s, pl.ds(c * wide + k, 1), :] for s in range(2) for c in range(3)
                ]
                total = total + contract(
                    spread(parts, row_of_entry[pl.ds(k, 1), :], own_rows), lane_hot[k]
                )
            acc_e[...] = total

        contact = jnp.zeros((6 * own_rows, LANES), jnp.float32)
        groups = plane_rows // chunks
        for j in range(PLANES - 1, -1, -1):
            if j == 0:
                halo_wait(back)
                values = [
                    jnp.concatenate([halo_side(back, 0, c), halo_side(back, 1, c)], axis=1)
                    for c in range(3)
                ]
                halves = [split(-value) for value in values]
                parts = [halves[c][s] for s in range(2) for c in range(3)]
                contact = contact + contract(
                    spread(parts, row_of_entry[lend : lend + 1, :], own_rows), lane_hot[lend]
                )
            box_wait(back, j)
            for m in range(groups):
                boxes = []
                for i in range(chunks):
                    q = (m * chunks + i) * per_row
                    boxes.append(
                        box_row(back, [device_at(j, q + t) for t in range(per_row)])
                    )
                halves = split(jnp.concatenate(boxes, axis=1))
                parts = [halves[s][c : c + 1, :] for s in range(2) for c in range(3)]
                k = first_slot + j * groups + m
                contact = contact + contract(
                    spread(parts, row_of_entry[k : k + 1, :], own_rows), lane_hot[k]
                )

        total = contact - acc_e[...]
        total = total[: 3 * own_rows] + total[3 * own_rows :]
        for c in range(3):
            rows = slice(c * own_rows, (c + 1) * own_rows)
            acceleration = (loads[rows, :] + total[rows]) / mass[...]
            now = cur[rows, :]
            later = 2.0 * now - old[rows, :] + time_step_sq * acceleration
            if step == STEPS - 1:
                out_u[rows, :] = later
                out_a[rows, :] = acceleration
            else:
                old[rows, :] = now
                cur[rows, :] = later

    for i in range(2 * STEPS):
        box_bytes(i, n - 1, 0).wait_send()
        for copy in halo_copies(i):
            copy.wait_send()


def on_device(
    n_py,
    displacement,
    disp_prev,
    nodal_load,
    nodal_mass,
    modulus,
    stiffness,
    connectivity,
    ghost_send,
    contact_node,
    contact_owner,
    pair_ids,
    gap_start,
    penalty,
    friction,
    slip_state,
):
    n = lax.axis_size(("px", "py"))
    cap = 2 * contact_node.shape[0] // n
    elnode, width = connectivity.shape
    nodes = displacement.shape[1]
    lent = ghost_send.shape[1]
    own_rows = nodes // LANES
    slot_rows = n * cap // LANES
    wide = -(-elnode // SUBLANES) * SUBLANES
    pair_rows = pair_ids.shape[1] // LANES
    slot_groups = slot_rows * LANES // width
    pair_groups = pair_ids.shape[1] // width
    inner = width * 3 // 4
    entries = elnode + 1 + 2 * pair_groups + slot_groups
    flat = (3 * own_rows, LANES)
    vmem = pl.BlockSpec(memory_space=pltpu.VMEM)
    hbm = pl.BlockSpec(memory_space=pltpu.HBM)
    f32, bf16, i32 = jnp.float32, jnp.bfloat16, jnp.int32
    dma = pltpu.SemaphoreType.DMA
    args = [
        displacement,
        disp_prev,
        nodal_load,
        nodal_mass.reshape(-1, LANES),
        modulus.reshape(1, -1),
        stiffness,
        connectivity,
        ghost_send,
        contact_node.reshape(-1, LANES),
        contact_owner.reshape(-1, LANES),
        pair_ids,
        gap_start,
        penalty.reshape(-1, LANES),
        friction.reshape(-1, LANES),
        slip_state,
    ]
    new_u, acc = pl.pallas_call(
        functools.partial(kernel, (n_py, n, cap, elnode, lent, width, inner)),
        out_shape=[jax.ShapeDtypeStruct(flat, f32)] * 2,
        in_specs=[hbm] * len(args),
        out_specs=[vmem] * 2,
        scratch_shapes=[pltpu.VMEM(a.shape, a.dtype) for a in args]
        + [
            pltpu.VMEM((entries, width), i32),
            pltpu.VMEM((entries, LANES, width), bf16),
            pltpu.VMEM((3 * wide, 9 * wide), f32),
            pltpu.VMEM((slot_rows, LANES), i32),
            pltpu.VMEM((2 * pair_rows, LANES), i32),
            pltpu.VMEM((SUBLANES, LANES), i32),
            pltpu.VMEM((3 * wide, width), f32),
            pltpu.VMEM((2, 3 * wide, width), f32),
            pltpu.VMEM((6 * own_rows, LANES), f32),
            pltpu.VMEM(flat, f32),
            pltpu.VMEM(flat, f32),
            pltpu.VMEM(flat, f32),
            pltpu.VMEM((3 * pair_rows, LANES), f32),
            pltpu.VMEM((3 * pair_rows, LANES), i32),
            pltpu.VMEM((2 * STEPS, n, 3, cap), f32),
            pltpu.VMEM((2 * STEPS, n, 3, cap), f32),
            pltpu.VMEM((2 * STEPS, 2, 3, lent), f32),
            pltpu.VMEM((2 * STEPS, 2, 3, lent), f32),
            dma((len(args),)),
            dma((2 * STEPS,)),
            dma((2 * STEPS, PLANES)),
            dma((2 * STEPS, 2)),
            dma((2 * STEPS, 2)),
        ],
        compiler_params=pltpu.CompilerParams(
            collective_id=0, has_side_effects=True, vmem_limit_bytes=48 * 1024 * 1024
        ),
        name="contact_steps",
    )(*args)
    return new_u.reshape(displacement.shape), acc.reshape(displacement.shape)


def solution(mesh):
    both = ("px", "py")
    row, cols = P(both), P(None, both)
    return jax.shard_map(
        functools.partial(on_device, mesh.shape["py"]),
        mesh=mesh,
        in_specs=(cols, cols, cols, row, row, P(), cols, cols, row, row, cols, cols, row, row, cols),
        out_specs=(cols, cols),
        check_vma=False,
    )
```

time: 60.8 us -> 54.3 us (0.89)
  Pallas kernels: 52.3 us -> 41.2 us
  local copies, waits for them, and re-layouts: 7.38 us -> 11.7 us
    pallas_call x1, Pallas kernels: 52.3 us -> 41.2 us  [on_device(): pl.pallas_call(functools.partial(kernel, (n_py, n, cap, elnode, lent, wid...]
    unnamed x23 -> x30, local copies, waits for them, and re-layouts: 3.11 us -> 10.4 us
    reshape x7 -> x0, local copies, waits for them, and re-layouts: 2.96 us -> none  [the longest x1 0.74 us: on_device(): pairs = pair_ids.reshape(-1, width)]
where the time goes in v1:
time: 54.3 us; the launch traced here: 53.6 us
  Pallas kernels  41.2 us (76%)
  local copies, waits for them, and re-layouts  11.7 us (22%)
  between operations  0.68 us (1%)
    pallas_call x1, Pallas kernels, on_device(): pl.pallas_call(functools.partial(kernel, (n_py, n, cap, elnode, lent, wid...  41.2 us
    unnamed x30, local copies, waits for them, and re-layouts  10.4 us
    reshape x2, local copies, waits for them, and re-layouts, on_device(): return (new_u.reshape(displacement.shape), acc.reshape(displacement.shape))  1.3 us

profile of v1, /device:TPU:0, one launch (start us, length us, event | category | flops | bytes accessed | tf_op | source)
XLA Modules:
  0.0 53.6 jit_solution(242597217502666335)
XLA Ops:
  0.6 0.0 copy-start.8
  0.6 0.0 copy-start.13
  0.7 0.7 %copy-done.8 = s32[2048]{0:T(1024)S(1)} copy-done((s32[2048]{0:T(1024)S(1)}, s32[2048]{0:T(1024)}, u32[]{:S(2)}) %copy-start.8) | copy-done | bytes 8216
  1.3 0.0 copy-done.13
  1.3 0.0 copy-start
  1.3 0.8 %copy-done = f32[3,4096]{1,0:T(4,128)S(1)} copy-done((f32[3,4096]{1,0:T(4,128)S(1)}, f32[3,4096]{1,0:T(4,128)}, u32[]{:S(2)}) %copy-start) | copy-done | bytes 49176
  2.2 0.0 copy-start.1
  2.2 0.8 %copy-done.1 = f32[3,4096]{1,0:T(4,128)S(1)} copy-done((f32[3,4096]{1,0:T(4,128)S(1)}, f32[3,4096]{1,0:T(4,128)}, u32[]{:S(2)}) %copy-start.1) | copy-done | bytes 49176
  3.0 0.0 copy-start.2
  3.0 0.8 %copy-done.2 = f32[3,4096]{1,0:T(4,128)S(1)} copy-done((f32[3,4096]{1,0:T(4,128)S(1)}, f32[3,4096]{1,0:T(4,128)}, u32[]{:S(2)}) %copy-start.2) | copy-done | bytes 49176
  3.9 0.0 copy-start.3
  3.9 0.8 %copy-done.3 = s32[27,512]{1,0:T(8,128)S(1)} copy-done((s32[27,512]{1,0:T(8,128)S(1)}, s32[27,512]{1,0:T(8,128)}, u32[]{:S(2)}) %copy-start.3) | copy-done | bytes 55320
  4.7 0.0 copy-start.4
  4.7 0.8 %copy-done.4 = f32[81,81]{1,0:T(8,128)S(1)} copy-done((f32[81,81]{1,0:T(8,128)S(1)}, f32[81,81]{1,0:T(8,128)}, u32[]{:S(2)}) %copy-start.4) | copy-done | bytes 26268
  5.5 0.0 copy-start.5
  5.5 0.7 %copy-done.5 = f32[4096]{0:T(1024)S(1)} copy-done((f32[4096]{0:T(1024)S(1)}, f32[4096]{0:T(1024)}, u32[]{:S(2)}) %copy-start.5) | copy-done | bytes 16408
  6.2 0.0 copy-start.6
  6.2 0.7 %copy-done.6 = f32[3,1024]{1,0:T(4,128)S(1)} copy-done((f32[3,1024]{1,0:T(4,128)S(1)}, f32[3,1024]{1,0:T(4,128)}, u32[]{:S(2)}) %copy-start.6) | copy-done | bytes 12312
  6.9 0.0 copy-start.7
  6.9 0.7 %copy-done.7 = s32[3,1024]{1,0:T(4,128)S(1)} copy-done((s32[3,1024]{1,0:T(4,128)S(1)}, s32[3,1024]{1,0:T(4,128)}, u32[]{:S(2)}) %copy-start.7) | copy-done | bytes 12312
  7.6 0.7 %copy-done.9 = s32[2048]{0:T(1024)S(1)} copy-done((s32[2048]{0:T(1024)S(1)}, s32[2048]{0:T(1024)}, u32[]{:S(2)}) %copy-start.9) | copy-done | bytes 8216
  8.3 0.0 copy-start.10
  8.3 0.7 %copy-done.10 = s32[2,1024]{1,0:T(2,128)S(1)} copy-done((s32[2,1024]{1,0:T(2,128)S(1)}, s32[2,1024]{1,0:T(2,128)}, u32[]{:S(2)}) %copy-start.10) | copy-done | bytes 8216
  9.0 0.0 copy-start.11
  9.0 0.7 %copy-done.11 = f32[1024]{0:T(1024)S(1)} copy-done((f32[1024]{0:T(1024)S(1)}, f32[1024]{0:T(1024)}, u32[]{:S(2)}) %copy-start.11) | copy-done | bytes 4120
  9.7 0.0 copy-start.12
  9.7 0.7 %copy-done.12 = f32[1024]{0:T(1024)S(1)} copy-done((f32[1024]{0:T(1024)S(1)}, f32[1024]{0:T(1024)}, u32[]{:S(2)}) %copy-start.12) | copy-done | bytes 4120
  10.4 0.0 copy-start.14
  10.4 0.7 %copy-done.14 = s32[2,256]{1,0:T(2,128)S(1)} copy-done((s32[2,256]{1,0:T(2,128)S(1)}, s32[2,256]{1,0:T(2,128)}, u32[]{:S(2)}) %copy-start.14) | copy-done | bytes 2072
  11.1 41.2 %contact_steps.1 = (f32[96,128]{1,0:T(8,128)S(1)}, f32[96,128]{1,0:T(8,128)S(1)}) custom-call(f32[3,4096]{1,0:T(4,128)S(1)} %copy-done, f32[3,4096]{1,0:T(4,128)S(1)} %copy-done.1, f32[3,4096]{1,0:T(4,128)S(1)} %copy-done.2, f32[32,128]{1,0:T(8,128)S(1)} %bitcast.6, f32[1,512]{1,0:T(1,128)S(1)} %bitcast.11, f32[81,81]{1,0:T(8,128)S(1)} %copy-done.4, ...), custom_call_target="tpu_custom_call" | custom-call | tf_op jit(solution)/shard_map/contact_steps/pallas_call | solution.py:613
  52.3 0.7 %reshape.34 = f32[3,4096]{1,0:T(4,128)} reshape(f32[96,128]{1,0:T(8,128)S(1)} %get-tuple-element.4) | data formatting | bytes 98304 | tf_op jit(solution)/shard_map/reshape | solution.py:649
  52.9 0.7 %reshape.35 = f32[3,4096]{1,0:T(4,128)} reshape(f32[96,128]{1,0:T(8,128)S(1)} %get-tuple-element.5) | data formatting | bytes 98304 | tf_op jit(solution)/shard_map/reshape | solution.py:649
  (1 shorter events, 0.0 us)
Async XLA Ops:
  0.6 0.7 %copy-start.8 = (s32[2048]{0:T(1024)S(1)}, s32[2048]{0:T(1024)}, u32[]{:S(2)}) copy-start(s32[2048]{0:T(1024)} %param.23) | copy-start | bytes 24580
  0.6 0.7 %copy-start.13 = (f32[512]{0:T(512)S(1)}, f32[512]{0:T(512)}, u32[]{:S(2)}) copy-start(f32[512]{0:T(512)} %param.19) | copy-start | bytes 6148
  1.3 0.8 %copy-start = (f32[3,4096]{1,0:T(4,128)S(1)}, f32[3,4096]{1,0:T(4,128)}, u32[]{:S(2)}) copy-start(f32[3,4096]{1,0:T(4,128)} %disp_hbm.1) | copy-start | bytes 147460
  2.2 0.8 %copy-start.1 = (f32[3,4096]{1,0:T(4,128)S(1)}, f32[3,4096]{1,0:T(4,128)}, u32[]{:S(2)}) copy-start(f32[3,4096]{1,0:T(4,128)} %prev_hbm.1) | copy-start | bytes 147460
  3.0 0.8 %copy-start.2 = (f32[3,4096]{1,0:T(4,128)S(1)}, f32[3,4096]{1,0:T(4,128)}, u32[]{:S(2)}) copy-start(f32[3,4096]{1,0:T(4,128)} %load_hbm.1) | copy-start | bytes 147460
  3.9 0.8 %copy-start.3 = (s32[27,512]{1,0:T(8,128)S(1)}, s32[27,512]{1,0:T(8,128)}, u32[]{:S(2)}) copy-start(s32[27,512]{1,0:T(8,128)} %conn_hbm.1) | copy-start | bytes 165892
  4.7 0.8 %copy-start.4 = (f32[81,81]{1,0:T(8,128)S(1)}, f32[81,81]{1,0:T(8,128)}, u32[]{:S(2)}) copy-start(f32[81,81]{1,0:T(8,128)} %stiff_hbm.1) | copy-start | bytes 78736
  5.5 0.7 %copy-start.5 = (f32[4096]{0:T(1024)S(1)}, f32[4096]{0:T(1024)}, u32[]{:S(2)}) copy-start(f32[4096]{0:T(1024)} %param.18) | copy-start | bytes 49156
  6.2 0.7 %copy-start.6 = (f32[3,1024]{1,0:T(4,128)S(1)}, f32[3,1024]{1,0:T(4,128)}, u32[]{:S(2)}) copy-start(f32[3,1024]{1,0:T(4,128)} %gap_hbm.1) | copy-start | bytes 36868
  6.9 0.7 %copy-start.7 = (s32[3,1024]{1,0:T(4,128)S(1)}, s32[3,1024]{1,0:T(4,128)}, u32[]{:S(2)}) copy-start(s32[3,1024]{1,0:T(4,128)} %slip_hbm.1) | copy-start | bytes 36868
  7.6 0.7 %copy-start.9 = (s32[2048]{0:T(1024)S(1)}, s32[2048]{0:T(1024)}, u32[]{:S(2)}) copy-start(s32[2048]{0:T(1024)} %param.24) | copy-start | bytes 24580
  8.3 0.7 %copy-start.10 = (s32[2,1024]{1,0:T(2,128)S(1)}, s32[2,1024]{1,0:T(2,128)}, u32[]{:S(2)}) copy-start(s32[2,1024]{1,0:T(2,128)} %pair_hbm.1) | copy-start | bytes 24580
  9.0 0.7 %copy-start.11 = (f32[1024]{0:T(1024)S(1)}, f32[1024]{0:T(1024)}, u32[]{:S(2)}) copy-start(f32[1024]{0:T(1024)} %param.27) | copy-start | bytes 12292
  9.7 0.7 %copy-start.12 = (f32[1024]{0:T(1024)S(1)}, f32[1024]{0:T(1024)}, u32[]{:S(2)}) copy-start(f32[1024]{0:T(1024)} %param.28) | copy-start | bytes 12292
  10.4 0.7 %copy-start.14 = (s32[2,256]{1,0:T(2,128)S(1)}, s32[2,256]{1,0:T(2,128)}, u32[]{:S(2)}) copy-start(s32[2,256]{1,0:T(2,128)} %ghost_hbm.1) | copy-start | bytes 6148

commit v2 on v1

--- a/solution.py
+++ b/solution.py
@@ -154,14 +154,25 @@
 
     per_plane = n // PLANES
     rows_y = n_py // PLANES
+    rows_x = n // n_py // 2
     z, y = lax.div(py, rows_y), lax.rem(py, rows_y)
+    x, core = lax.div(px, 2), lax.rem(px, 2)
     half = lax.div(z, 2)
     plane_at = [3 * (1 - half), 2 - half, 1 + 4 * half - z, z]
-    my_q = px * rows_y + y
+    turns = sorted(
+        [(a, e, b) for a in range(rows_x) for e in range(2) for b in range(rows_y)],
+        key=lambda t: min(t[0], rows_x - t[0]) + min(t[2], rows_y - t[2]) + 1 - t[1],
+        reverse=True,
+    )
+    my_q = turns.index((0, 0, 0))
     my_p = (PLANES - 1) * per_plane + my_q
+    columns = [
+        (lax.rem(x + a, rows_x) * 2 + lax.rem(core + e, 2)) * n_py + lax.rem(y + b, rows_y)
+        for a, e, b in turns
+    ]
 
     def device_at(j, q):
-        return lax.div(q, rows_y) * n_py + plane_at[j] * rows_y + lax.rem(q, rows_y)
+        return columns[q] + plane_at[j] * rows_y
 
     own_rows = cur.shape[0] // 3
     slot_rows = slot_idx.shape[0]
@@ -199,7 +210,14 @@
         0,
         jnp.where(target_z == plane_at[1], 1, jnp.where(target_z == plane_at[2], 2, 3)),
     )
-    spot = target_j * per_plane + lax.div(target, n_py) * rows_y + lax.rem(target_py, rows_y)
+    target_px = lax.div(target, n_py)
+    a = lax.rem(lax.div(target_px, 2) - x + rows_x, rows_x)
+    e = lax.rem(lax.rem(target_px, 2) - core + 2, 2)
+    b = lax.rem(lax.rem(target_py, rows_y) - y + rows_y, rows_y)
+    turn = (a * 2 + e) * rows_y + b
+    spot = target_j * per_plane
+    for q, (a, e, b) in enumerate(turns):
+        spot = spot + jnp.where(turn == (a * 2 + e) * rows_y + b, q, 0)
     pieces = owner.shape[0]
     hot = [jnp.where(matches(spot[i : i + 1, :], n), 1.0, 0.0) for i in range(pieces)]
     counts = jnp.dot(
@@ -249,36 +267,40 @@
             at = side * lent_rows + r
             lend_idx[at : at + 1, :] = ghost[side : side + 1, r * LANES : (r + 1) * LANES]
 
-    def box_copy(i, there, spot_out):
+    def box_copy(i, there, spot_out, kind):
         return pltpu.make_async_remote_copy(
             src_ref=box_out.at[i, spot_out],
             dst_ref=box_in.at[i, me],
             send_sem=box_send.at[i],
-            recv_sem=box_recv.at[i, z],
+            recv_sem=box_recv.at[i, z, kind],
             device_id=place(there),
             device_id_type=MESH,
         )
 
-    def box_bytes(i, count, plane):
+    def box_bytes(i, count, plane, kind):
         every = pl.ds(0, count)
         return pltpu.make_async_remote_copy(
             src_ref=box_out.at[i, every],
             dst_ref=box_in.at[i, every],
             send_sem=box_send.at[i],
-            recv_sem=box_recv.at[i, plane],
+            recv_sem=box_recv.at[i, plane, kind],
             device_id=place(lax.rem(me + 1, n)),
             device_id_type=MESH,
         )
 
     def box_start(i, j, by_device):
-        for d in range(1 if j == PLANES - 1 else 0, per_plane):
-            q = lax.rem(my_q + d, per_plane)
-            there = device_at(j, q)
-            box_copy(i, there, there if by_device else j * per_plane + q).start()
-
-    def box_wait(i, j):
+        for q in range(per_plane):
+            if j < PLANES - 1 or q != my_q:
+                there = device_at(j, q)
+                spot_out = there if by_device else j * per_plane + q
+                box_copy(i, there, spot_out, 0 if q == 0 else 1).start()
+
+    def wait_first(i, j):
+        box_bytes(i, 1, plane_at[j], 0).wait_recv()
+
+    def wait_rest(i, j):
         own = 1 if j == PLANES - 1 else 0
-        box_bytes(i, per_plane - own, plane_at[j]).wait_recv()
+        box_bytes(i, per_plane - 1 - own, plane_at[j], 1).wait_recv()
 
     def halo_copies(i):
         copies = []
@@ -317,6 +339,22 @@
     for step in range(STEPS):
         going, back = 2 * step, 2 * step + 1
 
+        def send_plane(j):
+            row_of, lane_of = places_of(slot_idx[j * plane_rows : (j + 1) * plane_rows, :])
+            got = blank()
+            for r in range(own_rows):
+                pick(got, table_lines(cur, own_rows, r), row_of, lane_of, r)
+            for q in range(per_plane):
+                r, l = divmod(q * cap, LANES)
+                for c in range(3):
+                    box_out[going, j * per_plane + q, c : c + 1, :] = got[c][
+                        r : r + 1, l : l + cap
+                    ]
+            if step == 0 and j == 0:
+                pl.semaphore_wait(barrier, n - 1)
+            box_start(going, j, False)
+
+        send_plane(0)
         row_of, lane_of = places_of(lend_idx[...])
         got = blank()
         for r in range(own_rows):
@@ -328,22 +366,9 @@
                     halo_out[going, side, c : c + 1, r * LANES : (r + 1) * LANES] = got[c][
                         at : at + 1
                     ]
-        if step == 0:
-            pl.semaphore_wait(barrier, n - 1)
         halo_start(going)
-
-        for j in range(PLANES):
-            row_of, lane_of = places_of(slot_idx[j * plane_rows : (j + 1) * plane_rows, :])
-            got = blank()
-            for r in range(own_rows):
-                pick(got, table_lines(cur, own_rows, r), row_of, lane_of, r)
-            for q in range(per_plane):
-                r, l = divmod(q * cap, LANES)
-                for c in range(3):
-                    box_out[going, j * per_plane + q, c : c + 1, :] = got[c][
-                        r : r + 1, l : l + cap
-                    ]
-            box_start(going, j, False)
+        for j in range(1, PLANES):
+            send_plane(j)
         box_in[going, me] = box_out[going, my_p]
 
         if step == 0:
@@ -367,6 +392,7 @@
             to_rows(slips, slip, pair_rows)
             to_rows(old, prev, own_rows)
             to_rows(loads, load, own_rows)
+            mass[...] = 1.0 / mass[...]
             ue[...] = jnp.zeros_like(ue)
             stiff_parts[...] = jnp.zeros_like(stiff_parts)
             for c in range(3):
@@ -404,18 +430,22 @@
         pair_at = [places_of(pair_idx[i * pair_rows : (i + 1) * pair_rows, :]) for i in range(2)]
         ends = [blank(), blank()]
 
-        def pair_pick(j):
-            for q in range(0, per_plane, per_row):
-                devices = [device_at(j, q + t) for t in range(per_row)]
-                box = box_row(going, devices)
-                lines = [box[c : c + 1, :] for c in range(3)]
-                row = lax.div(devices[0], per_row)
-                for i in range(2):
-                    pick(ends[i], lines, *pair_at[i], row)
-
-        for j in range(PLANES - 1, 0, -1):
-            box_wait(going, j)
-            pair_pick(j)
+        def pair_pick(lines_of, row):
+            for i in range(2):
+                pick(ends[i], lines_of, *pair_at[i], row)
+
+        def pair_picks(j, places):
+            for q in places:
+                there = device_at(j, q)
+                pair_pick([box_in[going, there, c : c + 1, :] for c in range(3)], there)
+
+        if per_row == 1:
+            for j in range(PLANES - 1, 0, -1):
+                wait_first(going, j)
+                wait_rest(going, j)
+                pair_picks(j, range(per_plane))
+            wait_rest(going, 0)
+            pair_picks(0, range(1, per_plane))
 
         halo_wait(going)
         ghosts = [[halo_side(going, side, c) for c in range(3)] for side in range(2)]
@@ -436,29 +466,16 @@
                     ue[c * wide + top : c * wide + top + SUBLANES, spots] = got[c]
         forces(slice(inner, width))
 
-        edge = jnp.zeros((6 * ghost_rows, LANES), jnp.float32)
-        for first in range(0, elnode, chunks):
-            lefts, rights = [], []
-            for k in range(first, min(first + chunks, elnode)):
-                row = row_of_entry[k : k + 1, inner:] - own_rows
-                parts = [
-                    fe[s, c * wide + k : c * wide + k + 1, inner:] for s in range(2) for c in range(3)
-                ]
-                lefts.append(spread(parts, row, ghost_rows))
-                rights.append(lane_hot[k, :, inner:])
-            edge = edge + contract(
-                jnp.concatenate(lefts, axis=1), jnp.concatenate(rights, axis=1)
-            )
-        edge = edge[: 3 * ghost_rows] + edge[3 * ghost_rows :]
-        for c in range(3):
-            for side in range(2):
-                for r in range(lent_rows):
-                    at = c * ghost_rows + side * lent_rows + r
-                    halo_out[back, side, c : c + 1, r * LANES : (r + 1) * LANES] = edge[at : at + 1]
-        halo_start(back)
-
-        box_wait(going, 0)
-        pair_pick(0)
+        if per_row == 1:
+            wait_first(going, 0)
+            pair_picks(0, range(1))
+        else:
+            for j in range(PLANES):
+                wait_first(going, j)
+                wait_rest(going, j)
+            for r in range(slot_rows):
+                box = box_row(going, [r * per_row + t for t in range(per_row)])
+                pair_pick([box[c : c + 1, :] for c in range(3)], r)
         gap = [
             gaps[c * pair_rows : (c + 1) * pair_rows, :] + ends[1][c] - ends[0][c] for c in range(3)
         ]
@@ -488,6 +505,27 @@
             box_start(back, j, True)
         box_in[back, me] = box_out[back, me]
 
+        edge = jnp.zeros((6 * ghost_rows, LANES), jnp.float32)
+        for first in range(0, elnode, chunks):
+            lefts, rights = [], []
+            for k in range(first, min(first + chunks, elnode)):
+                row = row_of_entry[k : k + 1, inner:] - own_rows
+                parts = [
+                    fe[s, c * wide + k : c * wide + k + 1, inner:] for s in range(2) for c in range(3)
+                ]
+                lefts.append(spread(parts, row, ghost_rows))
+                rights.append(lane_hot[k, :, inner:])
+            edge = edge + contract(
+                jnp.concatenate(lefts, axis=1), jnp.concatenate(rights, axis=1)
+            )
+        edge = edge[: 3 * ghost_rows] + edge[3 * ghost_rows :]
+        for c in range(3):
+            for side in range(2):
+                for r in range(lent_rows):
+                    at = c * ghost_rows + side * lent_rows + r
+                    halo_out[back, side, c : c + 1, r * LANES : (r + 1) * LANES] = edge[at : at + 1]
+        halo_start(back)
+
         if step == 0:
             for m in range(slot_groups):
                 set_row(first_slot + m, flat_row(slot_idx, m * chunks))
@@ -508,53 +546,77 @@
                 )
             acc_e[...] = total
 
-        contact = jnp.zeros((6 * own_rows, LANES), jnp.float32)
         groups = plane_rows // chunks
+
+        def home(j, m, places):
+            boxes = []
+            for i in places:
+                q = (m * chunks + i) * per_row
+                boxes.append(box_row(back, [device_at(j, q + t) for t in range(per_row)]))
+            halves = split(jnp.concatenate(boxes, axis=1))
+            parts = [halves[s][c : c + 1, :] for s in range(2) for c in range(3)]
+            k = first_slot + j * groups + m
+            lanes = slice(places[0] * LANES, (places[-1] + 1) * LANES)
+            return contract(
+                spread(parts, row_of_entry[k : k + 1, lanes], own_rows), lane_hot[k, :, lanes]
+            )
+
+        if per_row > 1:
+            for j in range(PLANES):
+                wait_first(back, j)
+                wait_rest(back, j)
+        total = -acc_e[...]
         for j in range(PLANES - 1, -1, -1):
-            if j == 0:
-                halo_wait(back)
-                values = [
-                    jnp.concatenate([halo_side(back, 0, c), halo_side(back, 1, c)], axis=1)
-                    for c in range(3)
-                ]
-                halves = [split(-value) for value in values]
-                parts = [halves[c][s] for s in range(2) for c in range(3)]
-                contact = contact + contract(
-                    spread(parts, row_of_entry[lend : lend + 1, :], own_rows), lane_hot[lend]
-                )
-            box_wait(back, j)
+            if per_row == 1:
+                if j > 0:
+                    wait_first(back, j)
+                wait_rest(back, j)
             for m in range(groups):
-                boxes = []
-                for i in range(chunks):
-                    q = (m * chunks + i) * per_row
-                    boxes.append(
-                        box_row(back, [device_at(j, q + t) for t in range(per_row)])
-                    )
-                halves = split(jnp.concatenate(boxes, axis=1))
-                parts = [halves[s][c : c + 1, :] for s in range(2) for c in range(3)]
-                k = first_slot + j * groups + m
-                contact = contact + contract(
-                    spread(parts, row_of_entry[k : k + 1, :], own_rows), lane_hot[k]
-                )
-
-        total = contact - acc_e[...]
+                total = total + home(j, m, range(1 if j == 0 and m == 0 else 0, chunks))
+        halo_wait(back)
+        values = [
+            jnp.concatenate([halo_side(back, 0, c), halo_side(back, 1, c)], axis=1)
+            for c in range(3)
+        ]
+        halves = [split(-value) for value in values]
+        parts = [halves[c][s] for s in range(2) for c in range(3)]
+        total = total + contract(
+            spread(parts, row_of_entry[lend : lend + 1, :], own_rows), lane_hot[lend]
+        )
         total = total[: 3 * own_rows] + total[3 * own_rows :]
+        first_acc, first_u = [], []
         for c in range(3):
             rows = slice(c * own_rows, (c + 1) * own_rows)
-            acceleration = (loads[rows, :] + total[rows]) / mass[...]
+            first_acc.append((loads[rows, :] + total[rows]) * mass[...])
             now = cur[rows, :]
-            later = 2.0 * now - old[rows, :] + time_step_sq * acceleration
+            first_u.append(2.0 * now - old[rows, :] + time_step_sq * first_acc[c])
+            if step < STEPS - 1:
+                old[rows, :] = now
+        if per_row == 1:
+            wait_first(back, 0)
+        last = home(0, 0, range(1))
+        last = last[: 3 * own_rows] + last[3 * own_rows :]
+        for c in range(3):
+            rows = slice(c * own_rows, (c + 1) * own_rows)
+            change = last[rows] * mass[...]
+            later = first_u[c] + time_step_sq * change
             if step == STEPS - 1:
                 out_u[rows, :] = later
-                out_a[rows, :] = acceleration
+                out_a[rows, :] = first_acc[c] + change
             else:
-                old[rows, :] = now
                 cur[rows, :] = later
 
     for i in range(2 * STEPS):
-        box_bytes(i, n - 1, 0).wait_send()
+        box_bytes(i, n - 1, 0, 0).wait_send()
         for copy in halo_copies(i):
             copy.wait_send()
+
+
+def unflatten(rows, u, a, out_u, out_a):
+    for table, out in ((u, out_u), (a, out_a)):
+        for c in range(3):
+            for r in range(rows):
+                out[c : c + 1, r * LANES : (r + 1) * LANES] = table[c * rows + r : c * rows + r + 1, :]
 
 
 def on_device(
@@ -637,16 +699,22 @@
             pltpu.VMEM((2 * STEPS, 2, 3, lent), f32),
             dma((len(args),)),
             dma((2 * STEPS,)),
-            dma((2 * STEPS, PLANES)),
+            dma((2 * STEPS, PLANES, 2)),
             dma((2 * STEPS, 2)),
             dma((2 * STEPS, 2)),
         ],
         compiler_params=pltpu.CompilerParams(
-            collective_id=0, has_side_effects=True, vmem_limit_bytes=48 * 1024 * 1024
+            collective_id=0, has_side_effects=True, vmem_limit_bytes=67043328
         ),
         name="contact_steps",
     )(*args)
-    return new_u.reshape(displacement.shape), acc.reshape(displacement.shape)
+    return pl.pallas_call(
+        functools.partial(unflatten, own_rows),
+        out_shape=[jax.ShapeDtypeStruct(displacement.shape, f32)] * 2,
+        in_specs=[vmem] * 2,
+        out_specs=[vmem] * 2,
+        name="unflatten",
+    )(new_u, acc)
 
 
 def solution(mesh):

time: 54.3 us -> 43.6 us (0.80); the launches traced: 53.6 us -> 43.4 us
  local copies, waits for them, and re-layouts: 11.7 us -> 0 us
  Pallas kernels: 41.2 us -> 42.8 us
    unnamed x30 -> x0, local copies, waits for them, and re-layouts: 10.4 us -> none
    pallas_call x0 -> x1, Pallas kernels: none -> 1.54 us  [on_device(): pl.pallas_call(functools.partial(unflatten, own_rows), out_shape=[jax.Sha...]
    reshape x2 -> x0, local copies, waits for them, and re-layouts: 1.3 us -> none  [on_device(): return (new_u.reshape(displacement.shape), acc.reshape(displacement.shape))]
where the time goes in v2:
time: 43.6 us; the launch traced here: 43.4 us
  Pallas kernels  42.8 us (98%)
  between operations  0.64 us (1%)
    pallas_call x1, Pallas kernels, on_device(): pl.pallas_call(functools.partial(kernel, (n_py, n, cap, elnode, lent, wid...  41.2 us
    pallas_call x1, Pallas kernels, on_device(): pl.pallas_call(functools.partial(unflatten, own_rows), out_shape=[jax.Sha...  1.54 us

profile of v2, /device:TPU:0, one launch (start us, length us, event | category | flops | bytes accessed | tf_op | source)
XLA Modules:
  0.0 43.4 jit_solution(10676267455235817913)
XLA Ops:
  0.6 41.2 %contact_steps.1 = (f32[96,128]{1,0:T(8,128)}, f32[96,128]{1,0:T(8,128)}) custom-call(f32[3,4096]{1,0:T(4,128)} %disp_hbm.1, f32[3,4096]{1,0:T(4,128)} %prev_hbm.1, f32[3,4096]{1,0:T(4,128)} %load_hbm.1, f32[32,128]{1,0:T(8,128)} %bitcast.6, f32[1,512]{1,0:T(1,128)} %bitcast.11, f32[81,81]{1,0:T(8,128)} %stiff_hbm.1, s32[27,512]{1,0:T(8,128)} %conn_hbm.1, ...), custom_call_target="tpu_custom_call" | custom-call | tf_op jit(solution)/shard_map/contact_steps/pallas_call | solution.py:675
  41.9 1.5 %unflatten.1 = (f32[3,4096]{1,0:T(4,128)}, f32[3,4096]{1,0:T(4,128)}) custom-call(f32[96,128]{1,0:T(8,128)} %get-tuple-element.4.u, f32[96,128]{1,0:T(8,128)} %get-tuple-element.5.a), custom_call_target="tpu_custom_call" | custom-call | tf_op jit(solution)/shard_map/unflatten/pallas_call | solution.py:711

commit v3 on v2

--- a/solution.py
+++ b/solution.py
@@ -11,6 +11,7 @@
 LANES = 128
 SUBLANES = 8
 PLANES = 4
+KINDS = 2
 MESH = pl.DeviceIdType.MESH
 
 time_step_sq = 0.05
@@ -157,22 +158,32 @@
     rows_x = n // n_py // 2
     z, y = lax.div(py, rows_y), lax.rem(py, rows_y)
     x, core = lax.div(px, 2), lax.rem(px, 2)
-    half = lax.div(z, 2)
-    plane_at = [3 * (1 - half), 2 - half, 1 + 4 * half - z, z]
-    turns = sorted(
-        [(a, e, b) for a in range(rows_x) for e in range(2) for b in range(rows_y)],
-        key=lambda t: min(t[0], rows_x - t[0]) + min(t[2], rows_y - t[2]) + 1 - t[1],
-        reverse=True,
-    )
-    my_q = turns.index((0, 0, 0))
-    my_p = (PLANES - 1) * per_plane + my_q
+    plane_at = [PLANES - 1 - z, lax.rem(z + 2, PLANES), z + 1 - 2 * lax.rem(z, 2), z]
+    planes = [plane * rows_y for plane in plane_at]
+    turns = [(a, e, b) for a in range(rows_x) for e in range(2) for b in range(rows_y)]
     columns = [
-        (lax.rem(x + a, rows_x) * 2 + lax.rem(core + e, 2)) * n_py + lax.rem(y + b, rows_y)
+        (lax.rem(x + a, rows_x) * 2 + lax.rem(core + e, 2), lax.rem(y + b, rows_y))
         for a, e, b in turns
     ]
 
-    def device_at(j, q):
-        return columns[q] + plane_at[j] * rows_y
+    def hops(place):
+        j, (a, e, b) = place[0], turns[place[1]]
+        return PLANES - 1 - j + min(a, rows_x - a) + min(b, rows_y - b) + 1 - e
+
+    places = sorted(
+        [(j, t) for j in range(PLANES) for t in range(per_plane)], key=hops, reverse=True
+    )
+    kinds = [0 if hops(place) > hops(places[0]) - 2 else 1 for place in places]
+    my_p = places.index((PLANES - 1, 0))
+    members = [[p for p in range(n) if kinds[p] == kind] for kind in range(KINDS)]
+
+    def place_at(p):
+        j, t = places[p]
+        return {"px": columns[t][0], "py": columns[t][1] + planes[j]}
+
+    def device_at(p):
+        there = place_at(p)
+        return there["px"] * n_py + there["py"]
 
     own_rows = cur.shape[0] // 3
     slot_rows = slot_idx.shape[0]
@@ -214,10 +225,10 @@
     a = lax.rem(lax.div(target_px, 2) - x + rows_x, rows_x)
     e = lax.rem(lax.rem(target_px, 2) - core + 2, 2)
     b = lax.rem(lax.rem(target_py, rows_y) - y + rows_y, rows_y)
-    turn = (a * 2 + e) * rows_y + b
-    spot = target_j * per_plane
-    for q, (a, e, b) in enumerate(turns):
-        spot = spot + jnp.where(turn == (a * 2 + e) * rows_y + b, q, 0)
+    turn = target_j * per_plane + (a * 2 + e) * rows_y + b
+    spot = jnp.zeros_like(target)
+    for p, (j, t) in enumerate(places):
+        spot = jnp.where(turn == j * per_plane + t, p, spot)
     pieces = owner.shape[0]
     hot = [jnp.where(matches(spot[i : i + 1, :], n), 1.0, 0.0) for i in range(pieces)]
     counts = jnp.dot(
@@ -267,40 +278,34 @@
             at = side * lent_rows + r
             lend_idx[at : at + 1, :] = ghost[side : side + 1, r * LANES : (r + 1) * LANES]
 
-    def box_copy(i, there, spot_out, kind):
+    def box_copy(i, p, spot_out):
         return pltpu.make_async_remote_copy(
             src_ref=box_out.at[i, spot_out],
             dst_ref=box_in.at[i, me],
             send_sem=box_send.at[i],
-            recv_sem=box_recv.at[i, z, kind],
-            device_id=place(there),
+            recv_sem=box_recv.at[i, kinds[p]],
+            device_id=place_at(p),
             device_id_type=MESH,
         )
 
-    def box_bytes(i, count, plane, kind):
+    def box_bytes(i, count, kind):
         every = pl.ds(0, count)
         return pltpu.make_async_remote_copy(
             src_ref=box_out.at[i, every],
             dst_ref=box_in.at[i, every],
             send_sem=box_send.at[i],
-            recv_sem=box_recv.at[i, plane, kind],
+            recv_sem=box_recv.at[i, kind],
             device_id=place(lax.rem(me + 1, n)),
             device_id_type=MESH,
         )
 
-    def box_start(i, j, by_device):
-        for q in range(per_plane):
-            if j < PLANES - 1 or q != my_q:
-                there = device_at(j, q)
-                spot_out = there if by_device else j * per_plane + q
-                box_copy(i, there, spot_out, 0 if q == 0 else 1).start()
-
-    def wait_first(i, j):
-        box_bytes(i, 1, plane_at[j], 0).wait_recv()
-
-    def wait_rest(i, j):
-        own = 1 if j == PLANES - 1 else 0
-        box_bytes(i, per_plane - 1 - own, plane_at[j], 1).wait_recv()
+    def box_start(i, spots, by_device):
+        for p in spots:
+            if p != my_p:
+                box_copy(i, p, device_at(p) if by_device else p).start()
+
+    def box_wait(i, kind):
+        box_bytes(i, len([p for p in members[kind] if p != my_p]), kind).wait_recv()
 
     def halo_copies(i):
         copies = []
@@ -339,26 +344,29 @@
     for step in range(STEPS):
         going, back = 2 * step, 2 * step + 1
 
-        def send_plane(j):
-            row_of, lane_of = places_of(slot_idx[j * plane_rows : (j + 1) * plane_rows, :])
+        def send_block(table, slots, j):
+            row_of, lane_of = places_of(slots[j * SUBLANES : (j + 1) * SUBLANES, :])
             got = blank()
             for r in range(own_rows):
-                pick(got, table_lines(cur, own_rows, r), row_of, lane_of, r)
-            for q in range(per_plane):
-                r, l = divmod(q * cap, LANES)
+                pick(got, table_lines(table, own_rows, r), row_of, lane_of, r)
+            spots = range(j * SUBLANES * per_row, (j + 1) * SUBLANES * per_row)
+            for p in spots:
+                r, l = divmod(p * cap - j * SUBLANES * LANES, LANES)
                 for c in range(3):
-                    box_out[going, j * per_plane + q, c : c + 1, :] = got[c][
-                        r : r + 1, l : l + cap
-                    ]
+                    box_out[going, p, c : c + 1, :] = got[c][r : r + 1, l : l + cap]
             if step == 0 and j == 0:
                 pl.semaphore_wait(barrier, n - 1)
-            box_start(going, j, False)
-
-        send_plane(0)
-        row_of, lane_of = places_of(lend_idx[...])
+            box_start(going, spots, False)
+
+        send_block(cur, slot_idx, 0)
+        now_at = cur[...]
+        slots = slot_idx[...]
+        lent_at = places_of(lend_idx[...])
+        for j in range(1, slot_rows // SUBLANES):
+            send_block(now_at, slots, j)
         got = blank()
         for r in range(own_rows):
-            pick(got, table_lines(cur, own_rows, r), row_of, lane_of, r)
+            pick(got, table_lines(now_at, own_rows, r), *lent_at, r)
         for c in range(3):
             for side in range(2):
                 for r in range(lent_rows):
@@ -367,8 +375,6 @@
                         at : at + 1
                     ]
         halo_start(going)
-        for j in range(1, PLANES):
-            send_plane(j)
         box_in[going, me] = box_out[going, my_p]
 
         if step == 0:
@@ -434,45 +440,21 @@
             for i in range(2):
                 pick(ends[i], lines_of, *pair_at[i], row)
 
-        def pair_picks(j, places):
-            for q in places:
-                there = device_at(j, q)
+        def pair_picks(kind):
+            box_wait(going, kind)
+            for p in members[kind]:
+                there = device_at(p)
                 pair_pick([box_in[going, there, c : c + 1, :] for c in range(3)], there)
 
         if per_row == 1:
-            for j in range(PLANES - 1, 0, -1):
-                wait_first(going, j)
-                wait_rest(going, j)
-                pair_picks(j, range(per_plane))
-            wait_rest(going, 0)
-            pair_picks(0, range(1, per_plane))
-
-        halo_wait(going)
-        ghosts = [[halo_side(going, side, c) for c in range(3)] for side in range(2)]
-        for top in tops:
-            row_of, lane_of = places_of(conn[top : top + SUBLANES, inner:])
-            for b in range((width - inner) // LANES):
-                lanes = slice(b * LANES, (b + 1) * LANES)
-                spots = slice(inner + b * LANES, inner + (b + 1) * LANES)
-                got = [ue[c * wide + top : c * wide + top + SUBLANES, spots] for c in range(3)]
-                for side in range(2):
-                    for r in range(lent_rows):
-                        lines = [
-                            ghosts[side][c][:, r * LANES : (r + 1) * LANES] for c in range(3)
-                        ]
-                        at = own_rows + side * lent_rows + r
-                        pick(got, lines, row_of[:, lanes], lane_of[:, lanes], at)
-                for c in range(3):
-                    ue[c * wide + top : c * wide + top + SUBLANES, spots] = got[c]
-        forces(slice(inner, width))
+            for kind in range(KINDS - 1, 0, -1):
+                pair_picks(kind)
 
         if per_row == 1:
-            wait_first(going, 0)
-            pair_picks(0, range(1))
+            pair_picks(0)
         else:
-            for j in range(PLANES):
-                wait_first(going, j)
-                wait_rest(going, j)
+            for kind in range(KINDS):
+                box_wait(going, kind)
             for r in range(slot_rows):
                 box = box_row(going, [r * per_row + t for t in range(per_row)])
                 pair_pick([box[c : c + 1, :] for c in range(3)], r)
@@ -501,9 +483,27 @@
             for c in range(3):
                 at = c * slot_rows + r
                 box_out[back, g, c : c + 1, :] = total[at : at + 1, l : l + cap]
-        for j in range(PLANES):
-            box_start(back, j, True)
+        box_start(back, range(n), True)
         box_in[back, me] = box_out[back, me]
+
+        halo_wait(going)
+        ghosts = [[halo_side(going, side, c) for c in range(3)] for side in range(2)]
+        for top in tops:
+            row_of, lane_of = places_of(conn[top : top + SUBLANES, inner:])
+            for b in range((width - inner) // LANES):
+                lanes = slice(b * LANES, (b + 1) * LANES)
+                spots = slice(inner + b * LANES, inner + (b + 1) * LANES)
+                got = [ue[c * wide + top : c * wide + top + SUBLANES, spots] for c in range(3)]
+                for side in range(2):
+                    for r in range(lent_rows):
+                        lines = [
+                            ghosts[side][c][:, r * LANES : (r + 1) * LANES] for c in range(3)
+                        ]
+                        at = own_rows + side * lent_rows + r
+                        pick(got, lines, row_of[:, lanes], lane_of[:, lanes], at)
+                for c in range(3):
+                    ue[c * wide + top : c * wide + top + SUBLANES, spots] = got[c]
+        forces(slice(inner, width))
 
         edge = jnp.zeros((6 * ghost_rows, LANES), jnp.float32)
         for first in range(0, elnode, chunks):
@@ -546,43 +546,37 @@
                 )
             acc_e[...] = total
 
-        groups = plane_rows // chunks
-
-        def home(j, m, places):
-            boxes = []
-            for i in places:
-                q = (m * chunks + i) * per_row
-                boxes.append(box_row(back, [device_at(j, q + t) for t in range(per_row)]))
-            halves = split(jnp.concatenate(boxes, axis=1))
-            parts = [halves[s][c : c + 1, :] for s in range(2) for c in range(3)]
-            k = first_slot + j * groups + m
-            lanes = slice(places[0] * LANES, (places[-1] + 1) * LANES)
-            return contract(
-                spread(parts, row_of_entry[k : k + 1, lanes], own_rows), lane_hot[k, :, lanes]
-            )
-
-        if per_row > 1:
-            for j in range(PLANES):
-                wait_first(back, j)
-                wait_rest(back, j)
+        def home(rows):
+            lefts, rights = [], []
+            for at in range(0, len(rows), chunks):
+                boxes, spots, hots = [], [], []
+                for r in rows[at : at + chunks]:
+                    k, l = first_slot + r // chunks, r % chunks * LANES
+                    boxes.append(
+                        box_row(back, [device_at(r * per_row + t) for t in range(per_row)])
+                    )
+                    spots.append(row_of_entry[k : k + 1, l : l + LANES])
+                    hots.append(lane_hot[k, :, l : l + LANES])
+                halves = split(jnp.concatenate(boxes, axis=1))
+                parts = [halves[s][c : c + 1, :] for s in range(2) for c in range(3)]
+                lefts.append(spread(parts, jnp.concatenate(spots, axis=1), own_rows))
+                rights.append(jnp.concatenate(hots, axis=1))
+            return lefts, rights
+
+        def gathered(lefts, rights):
+            return contract(jnp.concatenate(lefts, axis=1), jnp.concatenate(rights, axis=1))
+
+        if per_row == 1:
+            start = -(-members[1][0] // chunks) * chunks
+            early, late = [*range(start, n), *range(members[1][0], start)], members[0]
+        else:
+            early, late = range(slot_rows - plane_rows, slot_rows), range(slot_rows - plane_rows)
+            box_wait(back, 0)
+        box_wait(back, 1)
         total = -acc_e[...]
-        for j in range(PLANES - 1, -1, -1):
-            if per_row == 1:
-                if j > 0:
-                    wait_first(back, j)
-                wait_rest(back, j)
-            for m in range(groups):
-                total = total + home(j, m, range(1 if j == 0 and m == 0 else 0, chunks))
-        halo_wait(back)
-        values = [
-            jnp.concatenate([halo_side(back, 0, c), halo_side(back, 1, c)], axis=1)
-            for c in range(3)
-        ]
-        halves = [split(-value) for value in values]
-        parts = [halves[c][s] for s in range(2) for c in range(3)]
-        total = total + contract(
-            spread(parts, row_of_entry[lend : lend + 1, :], own_rows), lane_hot[lend]
-        )
+        lefts, rights = home(early)
+        for left, right in zip(lefts, rights):
+            total = total + contract(left, right)
         total = total[: 3 * own_rows] + total[3 * own_rows :]
         first_acc, first_u = [], []
         for c in range(3):
@@ -593,8 +587,18 @@
             if step < STEPS - 1:
                 old[rows, :] = now
         if per_row == 1:
-            wait_first(back, 0)
-        last = home(0, 0, range(1))
+            box_wait(back, 0)
+        halo_wait(back)
+        lefts, rights = home(late)
+        values = [
+            jnp.concatenate([halo_side(back, 0, c), halo_side(back, 1, c)], axis=1)
+            for c in range(3)
+        ]
+        halves = [split(-value) for value in values]
+        parts = [halves[c][s] for s in range(2) for c in range(3)]
+        lefts.append(spread(parts, row_of_entry[lend : lend + 1, :], own_rows))
+        rights.append(lane_hot[lend])
+        last = gathered(lefts, rights)
         last = last[: 3 * own_rows] + last[3 * own_rows :]
         for c in range(3):
             rows = slice(c * own_rows, (c + 1) * own_rows)
@@ -607,7 +611,7 @@
                 cur[rows, :] = later
 
     for i in range(2 * STEPS):
-        box_bytes(i, n - 1, 0, 0).wait_send()
+        box_bytes(i, n - 1, 0).wait_send()
         for copy in halo_copies(i):
             copy.wait_send()
 
@@ -699,7 +703,7 @@
             pltpu.VMEM((2 * STEPS, 2, 3, lent), f32),
             dma((len(args),)),
             dma((2 * STEPS,)),
-            dma((2 * STEPS, PLANES, 2)),
+            dma((2 * STEPS, KINDS)),
             dma((2 * STEPS, 2)),
             dma((2 * STEPS, 2)),
         ],

time: 43.6 us -> 42.2 us (0.968)
  Pallas kernels: 42.8 us -> 41.3 us
    pallas_call x1, Pallas kernels: 41.2 us -> 39.8 us  [on_device(): pl.pallas_call(functools.partial(kernel, (n_py, n, cap, elnode, lent, wid...]
where the time goes in v3:
time: 42.2 us; the launch traced here: 42 us
  Pallas kernels  41.3 us (98%)
  between operations  0.64 us (2%)
    pallas_call x1, Pallas kernels, on_device(): pl.pallas_call(functools.partial(kernel, (n_py, n, cap, elnode, lent, wid...  39.8 us
    pallas_call x1, Pallas kernels, on_device(): pl.pallas_call(functools.partial(unflatten, own_rows), out_shape=[jax.Sha...  1.54 us

profile of v3, /device:TPU:0, one launch (start us, length us, event | category | flops | bytes accessed | tf_op | source)
XLA Modules:
  0.0 42.0 jit_solution(16272096873588796266)
XLA Ops:
  0.6 39.8 %contact_steps.1 = (f32[96,128]{1,0:T(8,128)}, f32[96,128]{1,0:T(8,128)}) custom-call(f32[3,4096]{1,0:T(4,128)} %disp_hbm.1, f32[3,4096]{1,0:T(4,128)} %prev_hbm.1, f32[3,4096]{1,0:T(4,128)} %load_hbm.1, f32[32,128]{1,0:T(8,128)} %bitcast.6, f32[1,512]{1,0:T(1,128)} %bitcast.11, f32[81,81]{1,0:T(8,128)} %stiff_hbm.1, s32[27,512]{1,0:T(8,128)} %conn_hbm.1, ...), custom_call_target="tpu_custom_call" | custom-call | tf_op jit(solution)/shard_map/contact_steps/pallas_call | solution.py:679
  40.4 1.5 %unflatten.1 = (f32[3,4096]{1,0:T(4,128)}, f32[3,4096]{1,0:T(4,128)}) custom-call(f32[96,128]{1,0:T(8,128)} %get-tuple-element.4.u, f32[96,128]{1,0:T(8,128)} %get-tuple-element.5.a), custom_call_target="tpu_custom_call" | custom-call | tf_op jit(solution)/shard_map/unflatten/pallas_call | solution.py:715

commit v4 on v3

--- a/solution.py
+++ b/solution.py
@@ -573,10 +573,7 @@
             early, late = range(slot_rows - plane_rows, slot_rows), range(slot_rows - plane_rows)
             box_wait(back, 0)
         box_wait(back, 1)
-        total = -acc_e[...]
-        lefts, rights = home(early)
-        for left, right in zip(lefts, rights):
-            total = total + contract(left, right)
+        total = gathered(*home(early)) - acc_e[...]
         total = total[: 3 * own_rows] + total[3 * own_rows :]
         first_acc, first_u = [], []
         for c in range(3):
@@ -678,7 +675,7 @@
     ]
     new_u, acc = pl.pallas_call(
         functools.partial(kernel, (n_py, n, cap, elnode, lent, width, inner)),
-        out_shape=[jax.ShapeDtypeStruct(flat, f32)] * 2,
+        out_shape=[pltpu.VMEM(flat, f32)] * 2,
         in_specs=[hbm] * len(args),
         out_specs=[vmem] * 2,
         scratch_shapes=[pltpu.VMEM(a.shape, a.dtype) for a in args]
@@ -708,7 +705,7 @@
             dma((2 * STEPS, 2)),
         ],
         compiler_params=pltpu.CompilerParams(
-            collective_id=0, has_side_effects=True, vmem_limit_bytes=67043328
+            collective_id=0, has_side_effects=True, vmem_limit_bytes=66781184
         ),
         name="contact_steps",
     )(*args)
@@ -717,6 +714,7 @@
         out_shape=[jax.ShapeDtypeStruct(displacement.shape, f32)] * 2,
         in_specs=[vmem] * 2,
         out_specs=[vmem] * 2,
+        compiler_params=pltpu.CompilerParams(vmem_limit_bytes=4 * 1024 * 1024),
         name="unflatten",
     )(new_u, acc)
 

time: 42.2 us -> 40.6 us (0.962)
  Pallas kernels: 41.3 us -> 39.7 us
    pallas_call x1, Pallas kernels: 1.54 us -> 0.72 us  [on_device(): pl.pallas_call(functools.partial(unflatten, own_rows), out_shape=[jax.Sha...]
    pallas_call x1, Pallas kernels: 39.8 us -> 39 us  [on_device(): pl.pallas_call(functools.partial(kernel, (n_py, n, cap, elnode, lent, wid...]
where the time goes in v4:
time: 40.6 us; the launch traced here: 40.4 us
  Pallas kernels  39.7 us (98%)
  between operations  0.64 us (2%)
    pallas_call x1, Pallas kernels, on_device(): pl.pallas_call(functools.partial(kernel, (n_py, n, cap, elnode, lent, wid...  39 us

profile of v4, /device:TPU:0, one launch (start us, length us, event | category | flops | bytes accessed | tf_op | source)
XLA Modules:
  0.0 40.4 jit_solution(9024169056624206990)
XLA Ops:
  0.6 39.0 %contact_steps.1 = (f32[96,128]{1,0:T(8,128)S(1)}, f32[96,128]{1,0:T(8,128)S(1)}) custom-call(f32[3,4096]{1,0:T(4,128)} %disp_hbm.1, f32[3,4096]{1,0:T(4,128)} %prev_hbm.1, f32[3,4096]{1,0:T(4,128)} %load_hbm.1, f32[32,128]{1,0:T(8,128)} %bitcast.6, f32[1,512]{1,0:T(1,128)} %bitcast.11, f32[81,81]{1,0:T(8,128)} %stiff_hbm.1, s32[27,512]{1,0:T(8,128)} %conn_hbm.1, ...), custom_call_target="tpu_custom_call" | custom-call | tf_op jit(solution)/shard_map/contact_steps/pallas_call | solution.py:676
  39.7 0.7 %unflatten.1 = (f32[3,4096]{1,0:T(4,128)}, f32[3,4096]{1,0:T(4,128)}) custom-call(f32[96,128]{1,0:T(8,128)S(1)} %get-tuple-element.4.u, f32[96,128]{1,0:T(8,128)S(1)} %get-tuple-element.5.a), custom_call_target="tpu_custom_call" | custom-call | tf_op jit(solution)/shard_map/unflatten/pallas_call | solution.py:712

commit v5 on v4

--- a/solution.py
+++ b/solution.py
@@ -142,17 +142,6 @@
             ]
         )
     ]
-    for fill in fills:
-        fill.start()
-
-    barrier = pltpu.get_barrier_semaphore()
-
-    @pl.loop(1, n)
-    def _(d):
-        pl.semaphore_signal(
-            barrier, inc=1, device_id=place(lax.rem(me + d, n)), device_id_type=MESH
-        )
-
     per_plane = n // PLANES
     rows_y = n_py // PLANES
     rows_x = n // n_py // 2
@@ -184,6 +173,13 @@
     def device_at(p):
         there = place_at(p)
         return there["px"] * n_py + there["py"]
+
+    barrier = pltpu.get_barrier_semaphore()
+    for p in range(n):
+        if p != my_p:
+            pl.semaphore_signal(barrier, inc=1, device_id=place_at(p), device_id_type=MESH)
+    for fill in fills:
+        fill.start()
 
     own_rows = cur.shape[0] // 3
     slot_rows = slot_idx.shape[0]

time: 40.6 us -> 40.4 us (level)
  no operation moved by 1% of the time
where the time goes in v5:
time: 40.4 us; the launch traced here: 40.2 us
  Pallas kernels  39.6 us (98%)
  between operations  0.64 us (2%)
    pallas_call x1, Pallas kernels, on_device(): pl.pallas_call(functools.partial(kernel, (n_py, n, cap, elnode, lent, wid...  38.9 us

profile of v5, /device:TPU:0, one launch (start us, length us, event | category | flops | bytes accessed | tf_op | source)
XLA Modules:
  0.0 40.2 jit_solution(6334532368204004214)
XLA Ops:
  0.6 38.9 %contact_steps.1 = (f32[96,128]{1,0:T(8,128)S(1)}, f32[96,128]{1,0:T(8,128)S(1)}) custom-call(f32[3,4096]{1,0:T(4,128)} %disp_hbm.1, f32[3,4096]{1,0:T(4,128)} %prev_hbm.1, f32[3,4096]{1,0:T(4,128)} %load_hbm.1, f32[32,128]{1,0:T(8,128)} %bitcast.6, f32[1,512]{1,0:T(1,128)} %bitcast.11, f32[81,81]{1,0:T(8,128)} %stiff_hbm.1, s32[27,512]{1,0:T(8,128)} %conn_hbm.1, ...), custom_call_target="tpu_custom_call" | custom-call | tf_op jit(solution)/shard_map/contact_steps/pallas_call | solution.py:672
  39.5 0.7 %unflatten.1 = (f32[3,4096]{1,0:T(4,128)}, f32[3,4096]{1,0:T(4,128)}) custom-call(f32[96,128]{1,0:T(8,128)S(1)} %get-tuple-element.4.u, f32[96,128]{1,0:T(8,128)S(1)} %get-tuple-element.5.a), custom_call_target="tpu_custom_call" | custom-call | tf_op jit(solution)/shard_map/unflatten/pallas_call | solution.py:708

commit v6 on v5

--- a/solution.py
+++ b/solution.py
@@ -358,7 +358,7 @@
         now_at = cur[...]
         slots = slot_idx[...]
         lent_at = places_of(lend_idx[...])
-        for j in range(1, slot_rows // SUBLANES):
+        for j in range(1, slot_rows // SUBLANES - 1):
             send_block(now_at, slots, j)
         got = blank()
         for r in range(own_rows):
@@ -371,6 +371,7 @@
                         at : at + 1
                     ]
         halo_start(going)
+        send_block(now_at, slots, slot_rows // SUBLANES - 1)
         box_in[going, me] = box_out[going, my_p]
 
         if step == 0:
@@ -437,23 +438,42 @@
                 pick(ends[i], lines_of, *pair_at[i], row)
 
         def pair_picks(kind):
-            box_wait(going, kind)
             for p in members[kind]:
                 there = device_at(p)
                 pair_pick([box_in[going, there, c : c + 1, :] for c in range(3)], there)
 
         if per_row == 1:
-            for kind in range(KINDS - 1, 0, -1):
-                pair_picks(kind)
-
+            box_wait(going, 1)
+            pair_picks(1)
+
+        if per_row > 1:
+            box_wait(going, 1)
+        box_wait(going, 0)
+        halo_wait(going)
         if per_row == 1:
             pair_picks(0)
         else:
-            for kind in range(KINDS):
-                box_wait(going, kind)
             for r in range(slot_rows):
                 box = box_row(going, [r * per_row + t for t in range(per_row)])
                 pair_pick([box[c : c + 1, :] for c in range(3)], r)
+        ghosts = [[halo_side(going, side, c) for c in range(3)] for side in range(2)]
+        for top in tops:
+            row_of, lane_of = places_of(conn[top : top + SUBLANES, inner:])
+            for b in range((width - inner) // LANES):
+                lanes = slice(b * LANES, (b + 1) * LANES)
+                spots = slice(inner + b * LANES, inner + (b + 1) * LANES)
+                got = [ue[c * wide + top : c * wide + top + SUBLANES, spots] for c in range(3)]
+                for side in range(2):
+                    for r in range(lent_rows):
+                        lines = [
+                            ghosts[side][c][:, r * LANES : (r + 1) * LANES] for c in range(3)
+                        ]
+                        at = own_rows + side * lent_rows + r
+                        pick(got, lines, row_of[:, lanes], lane_of[:, lanes], at)
+                for c in range(3):
+                    ue[c * wide + top : c * wide + top + SUBLANES, spots] = got[c]
+        forces(slice(inner, width))
+
         gap = [
             gaps[c * pair_rows : (c + 1) * pair_rows, :] + ends[1][c] - ends[0][c] for c in range(3)
         ]
@@ -481,25 +501,6 @@
                 box_out[back, g, c : c + 1, :] = total[at : at + 1, l : l + cap]
         box_start(back, range(n), True)
         box_in[back, me] = box_out[back, me]
-
-        halo_wait(going)
-        ghosts = [[halo_side(going, side, c) for c in range(3)] for side in range(2)]
-        for top in tops:
-            row_of, lane_of = places_of(conn[top : top + SUBLANES, inner:])
-            for b in range((width - inner) // LANES):
-                lanes = slice(b * LANES, (b + 1) * LANES)
-                spots = slice(inner + b * LANES, inner + (b + 1) * LANES)
-                got = [ue[c * wide + top : c * wide + top + SUBLANES, spots] for c in range(3)]
-                for side in range(2):
-                    for r in range(lent_rows):
-                        lines = [
-                            ghosts[side][c][:, r * LANES : (r + 1) * LANES] for c in range(3)
-                        ]
-                        at = own_rows + side * lent_rows + r
-                        pick(got, lines, row_of[:, lanes], lane_of[:, lanes], at)
-                for c in range(3):
-                    ue[c * wide + top : c * wide + top + SUBLANES, spots] = got[c]
-        forces(slice(inner, width))
 
         edge = jnp.zeros((6 * ghost_rows, LANES), jnp.float32)
         for first in range(0, elnode, chunks):

time: 40.4 us -> 40.4 us (level)
  no operation moved by 1% of the time
where the time goes in v6:
time: 40.4 us; the launch traced here: 40.2 us
  Pallas kernels  39.6 us (98%)
  between operations  0.64 us (2%)
    pallas_call x1, Pallas kernels, on_device(): pl.pallas_call(functools.partial(kernel, (n_py, n, cap, elnode, lent, wid...  38.8 us

profile of v6, /device:TPU:0, one launch (start us, length us, event | category | flops | bytes accessed | tf_op | source)
XLA Modules:
  0.0 40.2 jit_solution(9150583829226045757)
XLA Ops:
  0.6 38.8 %contact_steps.1 = (f32[96,128]{1,0:T(8,128)S(1)}, f32[96,128]{1,0:T(8,128)S(1)}) custom-call(f32[3,4096]{1,0:T(4,128)} %disp_hbm.1, f32[3,4096]{1,0:T(4,128)} %prev_hbm.1, f32[3,4096]{1,0:T(4,128)} %load_hbm.1, f32[32,128]{1,0:T(8,128)} %bitcast.6, f32[1,512]{1,0:T(1,128)} %bitcast.11, f32[81,81]{1,0:T(8,128)} %stiff_hbm.1, s32[27,512]{1,0:T(8,128)} %conn_hbm.1, ...), custom_call_target="tpu_custom_call" | custom-call | tf_op jit(solution)/shard_map/contact_steps/pallas_call | solution.py:673
  39.5 0.7 %unflatten.1 = (f32[3,4096]{1,0:T(4,128)}, f32[3,4096]{1,0:T(4,128)}) custom-call(f32[96,128]{1,0:T(8,128)S(1)} %get-tuple-element.4.u, f32[96,128]{1,0:T(8,128)S(1)} %get-tuple-element.5.a), custom_call_target="tpu_custom_call" | custom-call | tf_op jit(solution)/shard_map/unflatten/pallas_call | solution.py:709
